TPU v7x, 256 devices: a whole 4x4x8 slice. The times are simulated.
256 devices in a mesh: row: 16 (over y, x), col: 16 (over z, core).
Axes of the slice: x: 4, y: 4, z: 8, core: 2. Of those that a mesh axis runs over, the one named last changes fastest.
Arguments:
- diag_inv: float32 [2, 2048, 2048], P(None, 'col', 'row'), may hold values from -0.125 to 0.125
- cross_block: float32 [2048, 2048], P('row', 'col'), may hold values from -0.125 to 0.125
- coupling: float32 [2, 2048, 65536], P(None, 'row', 'col'), may hold values from -0.125 to 0.125
- panel_loads: float32 [2, 1024, 2048], P(None, 'row', 'col'), may hold values from -6 to 6
- rest_loads: float32 [1024, 65536], P('row', 'col'), may hold values from -6 to 6
Outputs:
- solved: float32 [2, 1024, 2048], P(None, None, 'row')
- rest_updated: float32 [1024, 65536], P('row', 'col')
All inputs are finite; a program needn't handle non-finite values.
Results may differ from a plain program's by a relative error of at most 0.00008.
Values sent between devices are 32-bit elements; how exact they have to be, the bound alone decides.
A program may use at most 128 MiB of HBM per device.

v0:
```python
import jax
import jax.numpy as jnp
from jax import lax
from jax.sharding import PartitionSpec as P


def product(left, right):
    return jnp.dot(left, right, precision=lax.Precision.HIGHEST, preferred_element_type=jnp.float32)


def local(diag_inv, cross_block, coupling, panel_loads, rest_loads):
    both_full = lax.all_gather(panel_loads, "row", axis=1, tiled=True)

    def solve_panel(loads_full, panel_index):
        partial_value = product(loads_full, diag_inv[panel_index])
        return lax.psum(partial_value, "col")

    upper_solved = solve_panel(both_full[1], 1)
    lower_local = panel_loads[0] - lax.psum_scatter(
        product(upper_solved, cross_block), "row", scatter_dimension=0, tiled=True
    )
    lower_full = lax.all_gather(lower_local, "row", axis=0, tiled=True)
    lower_solved = solve_panel(lower_full, 0)

    def apply_panel(current, solved_part, panel_index):
        return current - lax.psum_scatter(
            product(solved_part, coupling[panel_index]), "row", scatter_dimension=0, tiled=True
        )

    rest_updated = apply_panel(rest_loads, upper_solved, 1)
    rest_updated = apply_panel(rest_updated, lower_solved, 0)
    return (jnp.stack([lower_solved, upper_solved]), rest_updated)


def solution(mesh):
    in_specs = (
        P(None, "col", "row"),
        P("row", "col"),
        P(None, "row", "col"),
        P(None, "row", "col"),
        P("row", "col"),
    )
    out_specs = (P(None, None, "row"), P("row", "col"))
    return jax.shard_map(local, mesh=mesh, in_specs=in_specs, out_specs=out_specs, check_vma=False)
```

profile of v0, /device:TPU:1, one launch (start us, length us, event | category | flops | bytes accessed | tf_op | source)
XLA Modules:
  0.0 639.2 jit_solution(14545961122653395243)
XLA Ops:
  7.2 0.0 all-gather.2.cloned.1.call-start
  7.2 0.7 all-gather.2.cloned.1.call-update
  7.9 0.0 all-reduce.3.cloned.1.call-start
  8.0 52.6 %all-gather.2.cloned.1.call-done = f32[2,1024,128]{2,1,0:T(8,128)} async-done(((f32[2,64,128]{2,1,0:T(8,128)}), f32[2,1024,128]{2,1,0:T(8,128)}) %all-gather.2.cloned.1.call-update) | async-done | bytes 1048592 | tf_op jit(solution)/shard_map/all_gather | solution.py:12
  60.6 2.4 fusion.6
  63.0 0.0 all-reduce.3.cloned.1.call-update
  63.0 0.0 reduce-scatter.4.cloned.1.call-start
  63.0 110.8 %all-reduce.3.cloned.1.call-done = f32[1024,128]{1,0:T(8,128)} async-done(((f32[1024,128]{1,0:T(8,128)}), f32[1024,128]{1,0:T(8,128)}) %all-reduce.3.cloned.1.call-update) | async-done | bytes 524304 | tf_op jit(solution)/shard_map/psum | solution.py:16
  173.8 2.5 fusion.12
  176.3 0.0 all-reduce.5.cloned.1.call-start
  176.4 78.0 %reduce-scatter.4.cloned.1.call-done = f32[64,128]{1,0:T(8,128)} async-done(((f32[1024,128]{1,0:T(8,128)}), f32[64,128]{1,0:T(8,128)}) %reduce-scatter.4.cloned.1.call-update) | async-done | bytes 32784 | tf_op jit(solution)/shard_map/reduce_scatter | solution.py:19
  254.3 0.8 bitcast_subtract_fusion
  255.1 17.5 %all_gather.7 = f32[1024,128]{1,0:T(8,128)S(1)} all-gather(f32[64,128]{1,0:T(8,128)S(1)} %bitcast_subtract_fusion), channel_id=1, replica_groups=mesh['row'=16,'col'=16] {'row'}, dimensions={0}, use_global_device_ids=true | all-gather | bytes 557056 | tf_op jit(solution)/shard_map/all_gather | solution.py:22
  272.6 2.2 fusion.7
  274.8 0.0 reduce-scatter.6.cloned.1.call-start
  274.9 16.7 %fusion.2 = f32[1024,4096]{1,0:T(8,128)} fusion(f32[1024,128]{1,0:T(8,128)S(1)} %copy-done.1, f32[2,128,4096]{2,1,0:T(8,128)} %param.7), kind=kOutput, calls=%fused_computation.2 | convolution fusion | flops 6442450944 | bytes 19398656 | tf_op jit(solution)/shard_map/dot_general | solution.py:8
  291.6 0.0 reduce-scatter.8.cloned.1.call-start
  291.7 99.1 %all-reduce.5.cloned.1.call-done = f32[1024,128]{1,0:T(8,128)} async-done(((f32[1024,128]{1,0:T(8,128)}), f32[1024,128]{1,0:T(8,128)}) %all-reduce.5.cloned.1.call-update) | async-done | bytes 524304 | tf_op jit(solution)/shard_map/psum | solution.py:16
  390.8 17.1 %fusion = f32[1024,4096]{1,0:T(8,128)} fusion(f32[1024,128]{1,0:T(8,128)} %all-reduce.5.cloned.1.call-done, f32[2,128,4096]{2,1,0:T(8,128)} %param.7), kind=kOutput, calls=%fused_computation | convolution fusion | flops 6442450944 | bytes 19398656 | tf_op jit(solution)/shard_map/dot_general | solution.py:8
  407.9 1.0 copy-done.2
  408.9 1.0 pad_maximum_fusion
  410.0 100.4 %reduce-scatter.6.cloned.1.call-done = f32[64,4096]{1,0:T(8,128)} async-done(((f32[1024,4096]{1,0:T(8,128)}), f32[64,4096]{1,0:T(8,128)}) %reduce-scatter.6.cloned.1.call-update) | async-done | bytes 1048592 | tf_op jit(solution)/shard_map/reduce_scatter | solution.py:26
  510.4 119.3 %reduce-scatter.8.cloned.1.call-done = f32[64,4096]{1,0:T(8,128)} async-done(((f32[1024,4096]{1,0:T(8,128)}), f32[64,4096]{1,0:T(8,128)}) %reduce-scatter.8.cloned.1.call-update) | async-done | bytes 1048592 | tf_op jit(solution)/shard_map/reduce_scatter | solution.py:26
  629.7 2.7 subtract_subtract_fusion
  (11 shorter events, 0.1 us)
Async XLA Ops:
  7.2 166.6 %copy-start = (f32[128,128]{1,0:T(8,128)S(1)}, f32[128,128]{1,0:T(8,128)}, u32[]{:S(2)}) copy-start(f32[128,128]{1,0:T(8,128)} %param.6) | copy-start | bytes 196612
  7.2 53.4 %all-gather.2.cloned.1.call-start = ((), (), s32[]{:S(2)}) async-start(), calls=%async_computation.3 | async-start | bytes 1114112 | tf_op jit(solution)/shard_map/all_gather | solution.py:12
  7.9 165.9 %all-reduce.3.cloned.1.call-start = ((), (), s32[]{:S(2)}) async-start(), calls=%async_computation.4 | async-start | bytes 1048576 | tf_op jit(solution)/shard_map/psum | solution.py:16
  63.0 191.3 %reduce-scatter.4.cloned.1.call-start = ((), (), s32[]{:S(2)}) async-start(), calls=%async_computation.5 | async-start | bytes 557056 | tf_op jit(solution)/shard_map/reduce_scatter | solution.py:19
  173.8 101.1 %copy-start.1 = (f32[1024,128]{1,0:T(8,128)S(1)}, f32[1024,128]{1,0:T(8,128)}, u32[]{:S(2)}) copy-start(f32[1024,128]{1,0:T(8,128)} %all-reduce.3.cloned.1.call-done) | copy-start | bytes 1572868
  176.3 214.5 %all-reduce.5.cloned.1.call-start = ((), (), s32[]{:S(2)}) async-start(), calls=%async_computation.6 | async-start | bytes 1048576 | tf_op jit(solution)/shard_map/psum | solution.py:16
  274.8 235.6 %reduce-scatter.6.cloned.1.call-start = ((), (), s32[]{:S(2)}) async-start(), calls=%async_computation.7 | async-start | bytes 17825792 | tf_op jit(solution)/shard_map/reduce_scatter | solution.py:26
  291.6 338.1 %reduce-scatter.8.cloned.1.call-start = ((), (), s32[]{:S(2)}) async-start(), calls=%async_computation.8 | async-start | bytes 17825792 | tf_op jit(solution)/shard_map/reduce_scatter | solution.py:26
  407.9 1.1 copy-start.2
  407.9 221.9 %copy-start.3 = (f32[64,4096]{1,0:T(8,128)S(1)}, f32[64,4096]{1,0:T(8,128)}, u32[]{:S(2)}) copy-start(f32[64,4096]{1,0:T(8,128)} %param.9) | copy-start | bytes 3145732
Sparse Core Ops, SparseCore 0:
  10.5 50.0 all-gather.1
  63.5 110.3 all-reduce.2
  178.3 76.0 reduce-scatter.3
  274.9 115.7 all-reduce.4
  394.8 115.5 reduce-scatter.5
  514.4 115.2 reduce-scatter.7
where the time goes:
time: 640 us; the launch traced here: 639 us
  waiting for transfers between devices  561 us (88%)
  matrix products  40.9 us (6%)
  blocking collectives  17.5 us (3%)
  between operations  14.1 us (2%)
    reduce_scatter x2, waiting for transfers between devices, apply_panel(): lax.psum_scatter(product(solved_part, coupling[panel_index]), 'row', scat...  220 us
    psum x2, waiting for transfers between devices, solve_panel(): return lax.psum(partial_value, 'col')  210 us
    reduce_scatter x1, waiting for transfers between devices, local(): lax.psum_scatter(product(upper_solved, cross_block), 'row', scatter_dimen...  78 us
    all_gather x1, waiting for transfers between devices, local(): both_full = lax.all_gather(panel_loads, 'row', axis=1, tiled=True)  52.6 us
    dot_general x5, matrix products, product(): jnp.dot(left, right, precision=lax.Precision.HIGHEST, preferred_element_t...  40.9 us
    all_gather x1, blocking collectives, local(): lower_full = lax.all_gather(lower_local, 'row', axis=0, tiled=True)  17.5 us
  transfers between devices with their start and end apart: 6, of which 6 were waited for; matrix products, arithmetic and copies ran while one was open for 5% of the time, Pallas kernels for 0%

commit v1 on v0

v1 whole, which is shorter than its diff:
```python
import functools

import jax
import jax.numpy as jnp
from jax import lax
from jax.experimental import pallas as pl
from jax.experimental.pallas import tpu as pltpu
from jax.sharding import PartitionSpec as P

MESH = pl.DeviceIdType.MESH


def halves(value):
    high = value.astype(jnp.bfloat16)
    low = (value - high.astype(jnp.float32)).astype(jnp.bfloat16)
    return high, low


def product(left, right_halves):
    left_high, left_low = halves(left)
    right_high, right_low = right_halves
    dot = functools.partial(jnp.dot, preferred_element_type=jnp.float32)
    return dot(left_high, right_high) + (dot(left_low, right_high) + dot(left_high, right_low))


def chain_kernel(n, diag_ref, cross_ref, loads_ref, solved_ref, gathered, parts, arrived, send_sem, recv_sem):
    row, col = lax.axis_index("row"), lax.axis_index("col")

    barrier = pltpu.get_barrier_semaphore()

    @pl.loop(1, n)
    def _(step):
        pl.semaphore_signal(barrier, inc=1, device_id={"row": lax.rem(row + step, n)}, device_id_type=MESH)
        pl.semaphore_signal(barrier, inc=1, device_id={"col": lax.rem(col + step, n)}, device_id_type=MESH)

    pl.semaphore_wait(barrier, 2 * (n - 1))

    def copy(phase, axis, mine, peer, source, target):
        return pltpu.make_async_remote_copy(
            src_ref=source,
            dst_ref=target,
            send_sem=send_sem.at[phase, peer],
            recv_sem=recv_sem.at[phase, mine],
            device_id={axis: peer},
            device_id_type=MESH,
        )

    def arrive(phase, axis, peer, place):
        copy(phase, axis, peer, peer, place, place).wait_recv()

    def spread(phase, axis, mine, block, slots):
        @pl.loop(1, n)
        def _(step):
            copy(phase, axis, mine, lax.rem(mine + step, n), block, slots.at[mine]).start()

    def multiply(phase, axis, mine, slots, right, part, other_axis, other, landing):
        right_halves = halves(right)

        @pl.loop(0, n)
        def _(step):
            peer = lax.rem(mine + n - step, n)

            @pl.when(step > 0)
            def _():
                arrive(phase, axis, peer, slots.at[peer])

            part[peer] = product(slots[peer], right_halves)

            @pl.when(peer != other)
            def _():
                copy(phase + 1, other_axis, other, peer, part.at[peer], landing.at[other]).start()

    def total(phase, axis, mine, part, landing):
        def add(step, value):
            peer = lax.rem(mine + n - step, n)
            arrive(phase, axis, peer, landing.at[peer])
            return value + landing[peer]

        return lax.fori_loop(1, n, add, part[mine])

    gathered[0, row] = loads_ref[1]
    spread(0, "row", row, gathered.at[0, row], gathered.at[0])
    multiply(0, "row", row, gathered.at[0], diag_ref[1], parts.at[0], "col", col, arrived.at[0])
    solved_ref[1, col] = total(1, "col", col, parts.at[0], arrived.at[0])
    spread(2, "col", col, solved_ref.at[1, col], solved_ref.at[1])
    multiply(2, "col", col, solved_ref.at[1], cross_ref[...], parts.at[1], "row", row, arrived.at[1])
    gathered[1, row] = loads_ref[0] - total(3, "row", row, parts.at[1], arrived.at[1])
    spread(4, "row", row, gathered.at[1, row], gathered.at[1])
    multiply(4, "row", row, gathered.at[1], diag_ref[0], parts.at[2], "col", col, arrived.at[2])
    solved_ref[0, col] = total(5, "col", col, parts.at[2], arrived.at[2])
    spread(6, "col", col, solved_ref.at[0, col], solved_ref.at[0])

    @pl.loop(1, n)
    def _(step):
        peer = lax.rem(col + n - step, n)
        arrive(6, "col", peer, solved_ref.at[0, peer])

    for phase, axis, mine in enumerate_phases(row, col):
        @pl.loop(1, n)
        def _(step):
            peer = lax.rem(mine + step, n)
            block = gathered.at[0, 0]
            copy(phase, axis, mine, peer, block, block).wait_send()


def enumerate_phases(row, col):
    axes = ("row", "col", "col", "row", "row", "col", "col")
    return [(phase, axis, row if axis == "row" else col) for phase, axis in enumerate(axes)]


def solve_panels(n, diag_inv, cross_block, panel_loads):
    _, height, width = panel_loads.shape
    vmem = pl.BlockSpec(memory_space=pltpu.VMEM)
    block = (n, height, width)
    solved = pl.pallas_call(
        functools.partial(chain_kernel, n),
        out_shape=jax.ShapeDtypeStruct((2,) + block, jnp.float32),
        in_specs=[vmem] * 3,
        out_specs=vmem,
        scratch_shapes=[
            pltpu.VMEM((2,) + block, jnp.float32),
            pltpu.VMEM((3,) + block, jnp.float32),
            pltpu.VMEM((3,) + block, jnp.float32),
            pltpu.SemaphoreType.DMA((7, n)),
            pltpu.SemaphoreType.DMA((7, n)),
        ],
        compiler_params=pltpu.CompilerParams(
            collective_id=0, has_side_effects=True, vmem_limit_bytes=24 * 2**20
        ),
    )(diag_inv, cross_block, panel_loads)
    return solved.reshape(2, n * height, width)


def solution(mesh):
    n = mesh.shape["row"]

    def local(diag_inv, cross_block, coupling, panel_loads, rest_loads):
        solved = solve_panels(n, diag_inv, cross_block, panel_loads)
        left = jnp.concatenate([solved[0], solved[1]], axis=1)
        right = coupling.reshape(-1, coupling.shape[2])
        partial_rest = jnp.dot(left, right, precision=lax.Precision.HIGH, preferred_element_type=jnp.float32)
        rest_updated = rest_loads - lax.psum_scatter(partial_rest, "row", scatter_dimension=0, tiled=True)
        return solved, rest_updated

    in_specs = (
        P(None, "col", "row"),
        P("row", "col"),
        P(None, "row", "col"),
        P(None, "row", "col"),
        P("row", "col"),
    )
    out_specs = (P(None, None, "row"), P("row", "col"))
    return jax.shard_map(local, mesh=mesh, in_specs=in_specs, out_specs=out_specs, check_vma=False)
```

time: 640 us -> 241 us (0.38)
  waiting for transfers between devices: 561 us -> 116 us
  Pallas kernels: 0 us -> 92.4 us
  matrix products: 40.9 us -> 12.5 us
  blocking collectives: 17.5 us -> 0 us
    psum x2 -> x0, waiting for transfers between devices: 210 us -> none  [solve_panel(): return lax.psum(partial_value, 'col')]
    reduce_scatter x3 -> x1, waiting for transfers between devices: 298 us -> 116 us  [local(): lax.psum_scatter(partial_rest, 'row', scatter_dimension=0, tiled=True)]
    pallas_call x0 -> x1, Pallas kernels: none -> 92.4 us  [solve_panels(): pl.pallas_call(functools.partial(chain_kernel, n), out_shape=jax.ShapeDty...]
    all_gather x1 -> x0, waiting for transfers between devices: 52.6 us -> none  [local(): both_full = lax.all_gather(panel_loads, 'row', axis=1, tiled=True)]
    dot_general x5 -> x1, matrix products: 40.9 us -> 12.5 us  [local(): jnp.dot(left, right, precision=lax.Precision.HIGH, preferred_element_type...]
    all_gather x1 -> x0, blocking collectives: 17.5 us -> none  [local(): lower_full = lax.all_gather(lower_local, 'row', axis=0, tiled=True)]
  transfers between devices with their start and end apart: 6 -> 1, of which waited for: 6 -> 1; matrix products, arithmetic and copies ran while one was open for 5% -> 0% of each run, Pallas kernels for 0% -> 0%
where the time goes in v1:
time: 241 us
  waiting for transfers between devices  116 us (48%)
  Pallas kernels  92.4 us (38%)
  between operations  14.1 us (6%)
  matrix products  12.5 us (5%)
  local copies, waits for them, and re-layouts  3.62 us (2%)
    reduce_scatter x1, waiting for transfers between devices, local(): lax.psum_scatter(partial_rest, 'row', scatter_dimension=0, tiled=True)  116 us
    pallas_call x1, Pallas kernels, solve_panels(): pl.pallas_call(functools.partial(chain_kernel, n), out_shape=jax.ShapeDty...  92.4 us
    dot_general x1, matrix products, local(): jnp.dot(left, right, precision=lax.Precision.HIGH, preferred_element_type...  12.5 us
  transfers between devices with their start and end apart: 1, of which 1 were waited for; matrix products, arithmetic and copies ran while one was open for 0% of the time, Pallas kernels for 0%

profile of v1, /device:TPU:1, one launch (start us, length us, event | category | flops | bytes accessed | tf_op | source)
XLA Modules:
  0.0 240.6 jit_solution(3106306653802220257)
XLA Ops:
  7.2 0.0 reduce-scatter.2.cloned.1.call-start
  7.2 0.0 copy-start
  7.2 0.9 copy-done
  8.1 0.0 copy-start.1
  8.1 0.8 copy-done.1
  9.0 0.0 copy-start.2
  9.0 0.8 copy-done.2
  9.8 92.4 %shard_map.68 = f32[2,16,64,128]{3,2,1,0:T(8,128)S(1)} custom-call(f32[2,128,128]{2,1,0:T(8,128)S(1)} %copy-done, f32[128,128]{1,0:T(8,128)S(1)} %copy-done.1, f32[2,64,128]{2,1,0:T(8,128)S(1)} %copy-done.2), custom_call_target="tpu_custom_call" | custom-call | tf_op jit(solution)/shard_map/pallas_call | solution.py:115
  102.2 0.1 fusion.5
  102.3 12.5 %fusion = f32[1024,4096]{1,0:T(8,128)} fusion(f32[256,4096]{1,0:T(8,128)} %bitcast.6, f32[1024,128]{1,0:T(8,128)S(1)} %bitcast.8, f32[1024,128]{1,0:T(8,128)S(1)} %bitcast.7), kind=kOutput, calls=%fused_computation | convolution fusion | flops 6442713088 | bytes 22020096 | tf_op jit(solution)/shard_map/dot_general | solution.py:141
  114.8 0.0 copy-start.3
  114.8 0.0 reduce-scatter.2.cloned.1.call-update
  114.8 115.6 %reduce-scatter.2.cloned.1.call-done = f32[64,4096]{1,0:T(8,128)} async-done(((f32[1024,4096]{1,0:T(8,128)}), f32[64,4096]{1,0:T(8,128)}) %reduce-scatter.2.cloned.1.call-update) | async-done | bytes 1048592 | tf_op jit(solution)/shard_map/reduce_scatter | solution.py:142
  230.5 0.0 copy-done.3
  230.5 2.3 sub.3
  232.8 1.0 copy.8
Async XLA Ops:
  7.2 223.3 %reduce-scatter.2.cloned.1.call-start = ((), (), s32[]{:S(2)}) async-start(), calls=%async_computation.1 | async-start | bytes 17825792 | tf_op jit(solution)/shard_map/reduce_scatter | solution.py:142
  7.2 0.9 copy-start
  8.1 0.8 copy-start.1
  9.0 0.8 copy-start.2
  114.8 115.7 %copy-start.3 = (f32[64,4096]{1,0:T(8,128)S(1)}, f32[64,4096]{1,0:T(8,128)}, u32[]{:S(2)}) copy-start(f32[64,4096]{1,0:T(8,128)} %param.9) | copy-start | bytes 3145732
Sparse Core Ops, SparseCore 0:
  114.9 115.4 reduce-scatter.1

commit v2 on v0

v2 whole, which is shorter than its diff:
```python
import functools
import math

import jax
import jax.numpy as jnp
from jax import lax
from jax.experimental import pallas as pl
from jax.experimental.pallas import tpu as pltpu
from jax.sharding import PartitionSpec as P

MESH = pl.DeviceIdType.MESH


def halves(value):
    high = value.astype(jnp.bfloat16)
    low = (value - high.astype(jnp.float32)).astype(jnp.bfloat16)
    return high, low


def product(left_halves, right_halves):
    left_high, left_low = left_halves
    right_high, right_low = right_halves
    dot = functools.partial(jnp.dot, preferred_element_type=jnp.float32)
    return dot(left_high, right_high) + (dot(left_low, right_high) + dot(left_high, right_low))


def solve_kernel(
    dims,
    diag_hbm, cross_hbm, coupling_hbm, loads_hbm, rest_hbm,
    solved, out,
    diag, cross, loads, rest,
    gathered, part_up, land_up, part_cross, land_cross, lower, part_low, land_low,
    raw_x, raw_y, high_x, low_x, high_y, low_y,
    along_x, along_y, sum_x, land_x, sum_y, land_y, done_x, done_y, tile_x, tile_y,
    local_sem, s_swap, r_swap, s_a, r_a, s_b, r_b, s_c, r_c, s_d, r_d, s_e, r_e, s_f, r_f, s_g, r_g,
    s_px, r_px, s_py, r_py, s_deal, r_deal, s_ux, r_ux, s_uy, r_uy, s_lx, r_lx, s_ly, r_ly,
    s_sx, r_sx, s_sy, r_sy, s_tx, r_tx, s_ty, r_ty, s_out, r_out,
):
    rows, nx, ny, nz, height, width, qx, qy = dims
    half = nx // 2
    row, col = lax.axis_index("row"), lax.axis_index("col")
    y, x = lax.div(row, nx), lax.rem(row, nx)
    z, core = lax.div(col, 2), lax.rem(col, 2)
    parity, slot = lax.rem(row, 2), lax.div(row, 2)
    holder = parity == core
    sibling = 2 * z + 1 - core

    def send(source, target, send_sem, recv_sem, to_row, to_col):
        copy = pltpu.make_async_remote_copy(
            src_ref=source, dst_ref=target, send_sem=send_sem, recv_sem=recv_sem,
            device_id={"row": to_row, "col": to_col}, device_id_type=MESH,
        )
        copy.start()

    def arrive(place, recv_sem):
        pltpu.make_async_remote_copy(
            src_ref=place, dst_ref=place, send_sem=s_swap.at[0], recv_sem=recv_sem,
            device_id={"row": row, "col": sibling}, device_id_type=MESH,
        ).wait_recv()

    def sent(place, send_sem):
        pltpu.make_async_remote_copy(
            src_ref=place, dst_ref=place, send_sem=send_sem, recv_sem=r_swap.at[0],
            device_id={"row": row, "col": sibling}, device_id_type=MESH,
        ).wait_send()

    own_copies = [
        pltpu.make_async_copy(diag_hbm, diag.at[core], local_sem.at[0]),
        pltpu.make_async_copy(cross_hbm, cross.at[core], local_sem.at[1]),
        pltpu.make_async_copy(loads_hbm.at[0], loads.at[core], local_sem.at[2]),
        pltpu.make_async_copy(rest_hbm, rest, local_sem.at[3]),
        pltpu.make_async_copy(
            coupling_hbm.at[:, :, pl.ds(pl.multiple_of(x * qx, qx), qx)], raw_x.at[core, :, x], local_sem.at[4]
        ),
        pltpu.make_async_copy(
            coupling_hbm.at[:, :, pl.ds(pl.multiple_of(nx * qx + y * qy, qy), qy)], raw_y.at[core, :, y], local_sem.at[5]
        ),
    ]
    for copy in own_copies:
        copy.start()
    own_upper = pltpu.make_async_copy(loads_hbm.at[1], gathered.at[slot, core], local_sem.at[6])

    @pl.when(holder)
    def _():
        own_upper.start()

    barrier = pltpu.get_barrier_semaphore()

    @pl.loop(0, rows)
    def _(step):
        peer = lax.rem(row + step, rows)
        pl.semaphore_signal(barrier, inc=1, device_id={"row": peer, "col": sibling}, device_id_type=MESH)

        @pl.when(step > 0)
        def _():
            pl.semaphore_signal(barrier, inc=1, device_id={"row": peer, "col": col}, device_id_type=MESH)

    @pl.loop(1, nz)
    def _(step):
        peer = lax.rem(z + step, nz)
        pl.semaphore_signal(barrier, inc=1, device_id={"row": row, "col": 2 * peer + core}, device_id_type=MESH)

    pl.semaphore_wait(barrier, 2 * rows - 1 + nz - 1)

    send(diag_hbm, diag.at[core], s_swap.at[0], r_swap.at[0], row, sibling)

    @pl.loop(0, rows)
    def _(step):
        @pl.when(jnp.logical_or(step > 0, jnp.logical_not(holder)))
        def _():
            peer = lax.rem(row + step, rows)
            send(loads_hbm.at[1], gathered.at[slot, core], s_a.at[peer], r_a.at[slot, core], peer, 2 * z + parity)

    send(cross_hbm, cross.at[core], s_swap.at[1], r_swap.at[1], row, sibling)
    send(loads_hbm.at[0], loads.at[core], s_swap.at[2], r_swap.at[2], row, sibling)

    def to_z(part, place, step_slot, landing, s_sem, r_sem):
        @pl.when(step_slot != z)
        def _():
            send(place, landing.at[z], s_sem.at[step_slot], r_sem.at[z], row, 2 * step_slot + core)

    def total_z(part, landing, r_sem):
        def add(step, value):
            peer = lax.rem(z + nz - step, nz)
            arrive(landing.at[peer], r_sem.at[peer])
            return value + landing[peer]

        return lax.fori_loop(1, nz, add, part[z])

    def spread_z(panel, s_sem, r_sem):
        @pl.loop(1, nz)
        def _(step):
            peer = lax.rem(z + step, nz)
            place = solved.at[panel, z, core]
            send(place, place, s_sem.at[peer], r_sem.at[z], row, 2 * peer + core)

    own_copies[0].wait()
    arrive(diag.at[1 - core], r_swap.at[0])

    @pl.when(holder)
    def _():
        own_upper.wait()

    upper_diag = halves(diag[:, 1].reshape(2 * width, width))

    @pl.loop(0, nz)
    def _(step):
        block = lax.rem(slot + nz - step, nz)
        for source in (0, 1):
            @pl.when(jnp.logical_not(jnp.logical_and(2 * block + core == row, source == core)))
            def _():
                arrive(gathered.at[block, source], r_a.at[block, source])

        left = jnp.concatenate([gathered[block, 0], gathered[block, 1]], axis=1)
        part_up[block] = product(halves(left), upper_diag)
        to_z(part_up, part_up.at[block], block, land_up, s_b, r_b)

    @pl.loop(1, nx)
    def _(step):
        peer = lax.rem(x + step, nx)
        send(
            coupling_hbm.at[:, :, pl.ds(pl.multiple_of(peer * qx, qx), qx)], raw_x.at[core, :, x],
            s_px.at[peer], r_px.at[x], y * nx + peer, col,
        )

    @pl.loop(1, ny)
    def _(step):
        peer = lax.rem(y + step, ny)
        send(
            coupling_hbm.at[:, :, pl.ds(pl.multiple_of(nx * qx + peer * qy, qy), qy)], raw_y.at[core, :, y],
            s_py.at[peer], r_py.at[y], peer * nx + x, col,
        )

    solved[1, z, core] = total_z(part_up, land_up, r_b)
    spread_z(1, s_c, r_c)

    own_copies[1].wait()
    arrive(cross.at[1 - core], r_swap.at[1])
    cross_halves = halves(jnp.concatenate([cross[0], cross[1]], axis=1))

    @pl.loop(0, nz)
    def _(step):
        block = lax.rem(z + nz - step, nz)

        @pl.when(step > 0)
        def _():
            arrive(solved.at[1, block, core], r_c.at[block])

        upper = solved[1, block, core]
        along_x[1, x, block] = upper
        along_y[1, y, block] = upper
        part_cross[block] = product(halves(upper), cross_halves)
        owner = 2 * block + core

        @pl.when(owner != row)
        def _():
            send(part_cross.at[block], land_cross.at[row], s_d.at[block], r_d.at[row], owner, col)

    own_copies[2].wait()
    arrive(loads.at[1 - core], r_swap.at[2])

    @pl.when(holder)
    def _():
        def add(step, value):
            peer = lax.rem(row + rows - step, rows)
            arrive(land_cross.at[peer], r_d.at[peer])
            return value + land_cross[peer]

        summed = lax.fori_loop(1, rows, add, part_cross[slot])
        lower[slot] = jnp.concatenate([loads[0], loads[1]], axis=1) - summed

        @pl.loop(1, rows)
        def _(step):
            peer = lax.rem(row + step, rows)
            send(lower.at[slot], lower.at[slot], s_e.at[peer], r_e.at[slot], peer, col)

    own_copies[4].wait()
    own_copies[5].wait()

    @pl.loop(1, nx)
    def _(step):
        peer = lax.rem(x + step, nx)
        arrive(raw_x.at[core, :, peer], r_px.at[peer])

    send(raw_x.at[core], raw_x.at[core], s_deal.at[0], r_deal.at[0], row, sibling)

    @pl.loop(1, ny)
    def _(step):
        peer = lax.rem(y + step, ny)
        arrive(raw_y.at[core, :, peer], r_py.at[peer])

    send(raw_y.at[core], raw_y.at[core], s_deal.at[1], r_deal.at[1], row, sibling)

    lower_diag = halves(diag[:, 0].reshape(2 * width, width))

    @pl.loop(0, nz)
    def _(step):
        block = lax.rem(slot + nz - step, nz)

        @pl.when(2 * block + core != row)
        def _():
            arrive(lower.at[block], r_e.at[block])

        part_low[block] = product(halves(lower[block]), lower_diag)
        to_z(part_low, part_low.at[block], block, land_low, s_f, r_f)

    @pl.loop(1, nx)
    def _(step):
        peer = lax.rem(x + step, nx)
        send(along_x.at[1, x], along_x.at[1, x], s_ux.at[peer], r_ux.at[x], y * nx + peer, col)

    @pl.loop(1, ny)
    def _(step):
        peer = lax.rem(y + step, ny)
        send(along_y.at[1, y], along_y.at[1, y], s_uy.at[peer], r_uy.at[y], peer * nx + x, col)

    send(solved.at[1, :, core], solved.at[1, :, core], s_out.at[1], r_out.at[1], row, sibling)

    arrive(raw_x.at[1 - core], r_deal.at[0])
    arrive(raw_y.at[1 - core], r_deal.at[1])

    def split(raw, high, low, groups):
        @pl.loop(0, 4 * groups)
        def _(index):
            owner, panel, group = lax.div(index, 2 * groups), lax.rem(lax.div(index, groups), 2), lax.rem(index, groups)
            start = pl.multiple_of((panel * groups + group) * width, width)
            block_high, block_low = halves(raw[owner, panel, group])
            high[owner, pl.ds(start, width)] = block_high
            low[owner, pl.ds(start, width)] = block_low

    split(raw_x, high_x, low_x, nx)
    split(raw_y, high_y, low_y, ny)

    solved[0, z, core] = total_z(part_low, land_low, r_f)
    spread_z(0, s_g, r_g)

    @pl.loop(0, nz)
    def _(step):
        block = lax.rem(z + nz - step, nz)

        @pl.when(step > 0)
        def _():
            arrive(solved.at[0, block, core], r_g.at[block])

        found = solved[0, block, core]
        along_x[0, x, block] = found
        along_y[0, y, block] = found
        for distance in range(1, nx):
            peer = lax.rem(x + distance, nx)
            place = along_x.at[0, x, block]
            send(place, place, s_lx.at[peer, block], r_lx.at[x, block], y * nx + peer, col)
        for distance in range(1, ny):
            peer = lax.rem(y + distance, ny)
            place = along_y.at[0, y, block]
            send(place, place, s_ly.at[peer, block], r_ly.at[y, block], peer * nx + x, col)

    send(solved.at[0, :, core], solved.at[0, :, core], s_out.at[0], r_out.at[0], row, sibling)

    @pl.loop(1, nx)
    def _(step):
        peer = lax.rem(x + step, nx)
        arrive(along_x.at[1, peer], r_ux.at[peer])

    @pl.loop(1, ny)
    def _(step):
        peer = lax.rem(y + step, ny)
        arrive(along_y.at[1, peer], r_uy.at[peer])

    def tile_over_y(peer):
        start = peer * half
        for distance in range(1, nx):
            source = lax.rem(x + distance, nx)
            for offset in range(half):
                arrive(along_x.at[0, source, start + offset], r_lx.at[source, start + offset])
        left = halves(jnp.concatenate(
            [along_x[panel, group, pl.ds(start, half)].reshape(half * height, width) for panel in (0, 1) for group in range(nx)],
            axis=1,
        ))
        for owner in (0, 1):
            value = product(left, (high_x[owner], low_x[owner]))
            sum_x[peer, :, owner] = value.reshape(half, height, qx)

        @pl.when(peer != y)
        def _():
            send(sum_x.at[peer], land_x.at[y], s_sx.at[peer], r_sx.at[y], peer * nx + x, col)

    def tile_over_x(offset):
        for distance in range(1, ny):
            source = lax.rem(y + distance, ny)
            for group in range(ny):
                arrive(along_y.at[0, source, group * half + offset], r_ly.at[source, group * half + offset])
        for start in range(0, ny, half):
            left = halves(jnp.concatenate(
                [
                    jnp.concatenate([along_y[panel, group, (start + part) * half + offset] for part in range(half)], axis=0)
                    for panel in (0, 1) for group in range(ny)
                ],
                axis=1,
            ))
            for owner in (0, 1):
                value = product(left, (high_y[owner], low_y[owner]))
                sum_y[offset, pl.ds(start, half), owner] = value.reshape(half, height, qy)
        target = 2 * offset + core

        @pl.when(target != x)
        def _():
            send(sum_y.at[offset], land_y.at[x], s_sy.at[offset], r_sy.at[x], y * nx + target, col)

    @pl.loop(0, half)
    def _(step):
        tile_over_y(lax.rem(y + 1 + 2 * step, ny))
        tile_over_x(lax.rem(lax.div(x, 2) + 1 + step, half))
        tile_over_y(lax.rem(y + 2 + 2 * step, ny))

    own_copies[3].wait()

    @pl.loop(1, ny)
    def _(step):
        peer = lax.rem(y + step, ny)
        arrive(land_x.at[peer], r_sx.at[peer])

    for offset in range(half):
        for owner in (0, 1):
            value = sum_x[y, offset, owner]
            for distance in range(1, ny):
                value = value + land_x[lax.rem(y + distance, ny), offset, owner]
            target = 2 * offset + core
            here = jnp.logical_and(target == x, owner == core)
            done_x[offset, owner] = value

            @pl.when(jnp.logical_not(here))
            def _():
                send(
                    done_x.at[offset, owner], tile_x.at[x], s_tx.at[offset, owner], r_tx.at[x],
                    y * nx + target, 2 * z + owner,
                )

    @pl.when(holder)
    def _():
        @pl.loop(1, nx)
        def _(step):
            peer = lax.rem(x + step, nx)
            arrive(land_y.at[peer], r_sy.at[peer])

        for peer in range(ny):
            for owner in (0, 1):
                value = sum_y[lax.div(x, 2), peer, owner]
                for distance in range(1, nx):
                    value = value + land_y[lax.rem(x + distance, nx), peer, owner]
                done_y[peer, owner] = value

                @pl.when(jnp.logical_not(jnp.logical_and(peer == y, owner == core)))
                def _():
                    send(
                        done_y.at[peer, owner], tile_y.at[y], s_ty.at[peer, owner], r_ty.at[y],
                        peer * nx + x, 2 * z + owner,
                    )

        tile_x[x] = done_x[lax.div(x, 2), core]
        tile_y[y] = done_y[y, core]

    for group in range(nx):
        @pl.when(jnp.logical_not(jnp.logical_and(holder, group == x)))
        def _():
            arrive(tile_x.at[group], r_tx.at[group])

        columns = pl.ds(group * qx, qx)
        out[:, columns] = rest[:, columns] - tile_x[group]

    for group in range(ny):
        @pl.when(jnp.logical_not(jnp.logical_and(holder, group == y)))
        def _():
            arrive(tile_y.at[group], r_ty.at[group])

        columns = pl.ds(nx * qx + group * qy, qy)
        out[:, columns] = rest[:, columns] - tile_y[group]

    for panel in (0, 1):
        arrive(solved.at[panel, :, 1 - core], r_out.at[panel])

    sent(diag.at[core], s_swap.at[0])
    sent(cross.at[core], s_swap.at[1])
    sent(loads.at[core], s_swap.at[2])
    for panel in (0, 1):
        sent(solved.at[panel, :, core], s_out.at[panel])
    sent(raw_x.at[core], s_deal.at[0])
    sent(raw_y.at[core], s_deal.at[1])

    @pl.loop(0, rows)
    def _(step):
        @pl.when(jnp.logical_or(step > 0, jnp.logical_not(holder)))
        def _():
            sent(gathered.at[0, 0], s_a.at[lax.rem(row + step, rows)])

        @pl.when(jnp.logical_and(step > 0, holder))
        def _():
            sent(lower.at[0], s_e.at[lax.rem(row + step, rows)])

    @pl.loop(1, nz)
    def _(step):
        peer = lax.rem(z + step, nz)
        sent(part_up.at[0], s_b.at[peer])
        sent(part_up.at[0], s_c.at[peer])
        sent(part_low.at[0], s_f.at[peer])
        sent(part_low.at[0], s_g.at[peer])

    @pl.loop(0, nz)
    def _(block):
        @pl.when(2 * block + core != row)
        def _():
            sent(part_cross.at[0], s_d.at[block])

        for distance in range(1, nx):
            sent(along_x.at[0, 0, 0], s_lx.at[lax.rem(x + distance, nx), block])
        for distance in range(1, ny):
            sent(along_y.at[0, 0, 0], s_ly.at[lax.rem(y + distance, ny), block])

    @pl.loop(1, nx)
    def _(step):
        peer = lax.rem(x + step, nx)
        sent(raw_x.at[core, :, 0], s_px.at[peer])
        sent(along_x.at[1, 0], s_ux.at[peer])

    @pl.loop(1, ny)
    def _(step):
        peer = lax.rem(y + step, ny)
        sent(raw_y.at[core, :, 0], s_py.at[peer])
        sent(along_y.at[1, 0], s_uy.at[peer])
        sent(sum_x.at[0], s_sx.at[peer])

    @pl.loop(0, half)
    def _(offset):
        target = 2 * offset + core

        @pl.when(target != x)
        def _():
            sent(sum_y.at[0], s_sy.at[offset])

        for owner in (0, 1):
            @pl.when(jnp.logical_not(jnp.logical_and(target == x, owner == core)))
            def _():
                sent(done_x.at[0, 0], s_tx.at[offset, owner])

    @pl.when(holder)
    def _():
        @pl.loop(0, ny)
        def _(peer):
            for owner in (0, 1):
                @pl.when(jnp.logical_not(jnp.logical_and(peer == y, owner == core)))
                def _():
                    sent(done_y.at[0, 0], s_ty.at[peer, owner])


def local(mesh, diag_inv, cross_block, coupling, panel_loads, rest_loads):
    rows, cols = mesh.shape["row"], mesh.shape["col"]
    nx = ny = math.isqrt(rows)
    nz, half = cols // 2, math.isqrt(rows) // 2
    _, height, width = panel_loads.shape
    span = rest_loads.shape[1]
    qx, qy = span // 2 // nx, span // 2 // ny
    f32, bf16 = jnp.float32, jnp.bfloat16
    vmem, dma = pltpu.VMEM, lambda *shape: pltpu.SemaphoreType.DMA(shape)
    block = (height, width)
    whole = pl.BlockSpec(memory_space=pltpu.VMEM)
    solved, rest_updated = pl.pallas_call(
        functools.partial(solve_kernel, (rows, nx, ny, nz, height, width, qx, qy)),
        out_shape=(
            jax.ShapeDtypeStruct((2, nz, 2) + block, f32),
            jax.ShapeDtypeStruct((height, span), f32),
        ),
        in_specs=[pl.BlockSpec(memory_space=pl.ANY)] * 5,
        out_specs=(whole, whole),
        scratch_shapes=[
            vmem((2, 2, width, width), f32),
            vmem((2, width, width), f32),
            vmem((2,) + block, f32),
            vmem((height, span), f32),
            vmem((nz, 2) + block, f32),
            vmem((nz,) + block, f32),
            vmem((nz,) + block, f32),
            vmem((nz, height, 2 * width), f32),
            vmem((rows, height, 2 * width), f32),
            vmem((nz, height, 2 * width), f32),
            vmem((nz,) + block, f32),
            vmem((nz,) + block, f32),
            vmem((2, 2, nx, width, qx), f32),
            vmem((2, 2, ny, width, qy), f32),
            vmem((2, 2 * nx * width, qx), bf16),
            vmem((2, 2 * nx * width, qx), bf16),
            vmem((2, 2 * ny * width, qy), bf16),
            vmem((2, 2 * ny * width, qy), bf16),
            vmem((2, nx, nz) + block, f32),
            vmem((2, ny, nz) + block, f32),
            vmem((ny, half, 2, height, qx), f32),
            vmem((ny, half, 2, height, qx), f32),
            vmem((half, ny, 2, height, qy), f32),
            vmem((nx, ny, 2, height, qy), f32),
            vmem((half, 2, height, qx), f32),
            vmem((ny, 2, height, qy), f32),
            vmem((nx, height, qx), f32),
            vmem((ny, height, qy), f32),
            dma(7), dma(3), dma(3),
            dma(rows), dma(nz, 2),
            dma(nz), dma(nz), dma(nz), dma(nz),
            dma(nz), dma(rows), dma(rows), dma(nz),
            dma(nz), dma(nz), dma(nz), dma(nz),
            dma(nx), dma(nx), dma(ny), dma(ny), dma(2), dma(2),
            dma(nx), dma(nx), dma(ny), dma(ny),
            dma(nx, nz), dma(nx, nz), dma(ny, nz), dma(ny, nz),
            dma(ny), dma(ny), dma(half), dma(nx),
            dma(half, 2), dma(nx), dma(ny, 2), dma(ny),
            dma(2), dma(2),
        ],
        compiler_params=pltpu.CompilerParams(
            collective_id=0, has_side_effects=True, vmem_limit_bytes=56 * 2**20
        ),
    )(diag_inv, cross_block, coupling, panel_loads, rest_loads)
    return solved.reshape(2, rows * height, width), rest_updated


def solution(mesh):
    in_specs = (
        P(None, "col", "row"),
        P("row", "col"),
        P(None, "row", "col"),
        P(None, "row", "col"),
        P("row", "col"),
    )
    out_specs = (P(None, None, "row"), P("row", "col"))
    return jax.shard_map(
        functools.partial(local, mesh), mesh=mesh, in_specs=in_specs, out_specs=out_specs, check_vma=False
    )
```

time: 640 us -> 133 us (0.21)
  waiting for transfers between devices: 561 us -> 0 us
  Pallas kernels: 0 us -> 128 us
  matrix products: 40.9 us -> 0 us
  blocking collectives: 17.5 us -> 0 us
  between operations: 14.1 us -> 0.64 us
    reduce_scatter x3 -> x0, waiting for transfers between devices: 298 us -> none  [the longest x2 220 us: apply_panel(): lax.psum_scatter(product(solved_part, coupling[panel_index]), 'row', scat...]
    psum x2 -> x0, waiting for transfers between devices: 210 us -> none  [solve_panel(): return lax.psum(partial_value, 'col')]
    pallas_call x0 -> x1, Pallas kernels: none -> 128 us  [local(): pl.pallas_call(functools.partial(solve_kernel, (rows, nx, ny, nz, height,...]
    all_gather x1 -> x0, waiting for transfers between devices: 52.6 us -> none  [local(): both_full = lax.all_gather(panel_loads, 'row', axis=1, tiled=True)]
    dot_general x5 -> x0, matrix products: 40.9 us -> none  [product(): jnp.dot(left, right, precision=lax.Precision.HIGHEST, preferred_element_t...]
    all_gather x1 -> x0, blocking collectives: 17.5 us -> none  [local(): lower_full = lax.all_gather(lower_local, 'row', axis=0, tiled=True)]
  transfers between devices with their start and end apart: 6 -> 0, of which waited for: 6 -> 0; matrix products, arithmetic and copies ran while one was open for 5% -> 0% of each run, Pallas kernels for 0% -> 0%
where the time goes in v2:
time: 133 us
  Pallas kernels  128 us (96%)
  local copies, waits for them, and re-layouts  4.53 us (3%)
    pallas_call x1, Pallas kernels, local(): pl.pallas_call(functools.partial(solve_kernel, (rows, nx, ny, nz, height,...  128 us
    unnamed x2, local copies, waits for them, and re-layouts  4.53 us

profile of v2, /device:TPU:1, one launch (start us, length us, event | category | flops | bytes accessed | tf_op | source)
XLA Modules:
  0.0 132.9 jit_solution(3442585222970576260)
XLA Ops:
  0.6 127.7 %shard_map.68 = (f32[2,8,2,64,128]{4,3,2,1,0:T(8,128)}, f32[64,4096]{1,0:T(8,128)}) custom-call(f32[2,128,128]{2,1,0:T(8,128)} %diag_hbm.1, f32[128,128]{1,0:T(8,128)} %cross_hbm.1, f32[2,128,4096]{2,1,0:T(8,128)} %coupling_hbm.1, f32[2,64,128]{2,1,0:T(8,128)} %loads_hbm.1, f32[64,4096]{1,0:T(8,128)} %rest_hbm.1), custom_call_target="tpu_custom_call" | custom-call | tf_op jit(solution)/shard_map/pallas_call | solution.py:505
  128.3 2.3 %copy.9 = f32[2,1024,128]{2,1,0:T(8,128)} copy(f32[2,1024,128]{2,1,0:T(8,128)} %bitcast.1) | data formatting | bytes 2097152
  130.6 2.3 %copy.10 = f32[64,4096]{1,0:T(8,128)} copy(f32[64,4096]{1,0:T(8,128)} %get-tuple-element.9) | data formatting | bytes 2097152

commit v3 on v2

v3 whole, which is shorter than its diff:
```python
import functools
import math

import jax
import jax.numpy as jnp
from jax import lax
from jax.experimental import pallas as pl
from jax.experimental.pallas import tpu as pltpu
from jax.sharding import PartitionSpec as P

MESH = pl.DeviceIdType.MESH


def halves(value):
    high = value.astype(jnp.bfloat16)
    low = (value - high.astype(jnp.float32)).astype(jnp.bfloat16)
    return high, low


def product(left_halves, right_halves):
    left_high, left_low = left_halves
    right_high, right_low = right_halves
    dot = functools.partial(jnp.dot, preferred_element_type=jnp.float32)
    return dot(left_high, right_high) + (dot(left_low, right_high) + dot(left_high, right_low))


def farthest_first(size):
    return sorted(range(1, size), key=lambda step: -min(step, size - step))


def solve_kernel(
    dims,
    diag_hbm, cross_hbm, coupling_hbm, loads_hbm, rest_hbm,
    solved, out,
    diag, cross, loads, rest,
    gathered, part_up, land_up, part_cross, land_cross, lower, part_low, land_low,
    raw_x, raw_y, high_x, low_x, high_y, low_y,
    along_x, along_y, sum_x, land_x, sum_y, land_y, done_x, done_y, tile_x, tile_y,
    local_sem, s_swap, r_swap, s_a, r_a, s_b, r_b, s_c, r_c, s_d, r_d, s_e, r_e, s_f, r_f, s_g, r_g,
    s_px, r_px, s_py, r_py, s_deal, r_deal, s_lx, r_lx, s_ly, r_ly,
    s_sx, r_sx, s_sy, r_sy, s_tx, r_tx, s_ty, r_ty, s_out, r_out,
):
    rows, nx, ny, nz, height, width, qx, qy = dims
    half, part = nx // 2, height // 2
    x_steps, y_steps, z_steps = farthest_first(nx), farthest_first(ny), farthest_first(nz)
    plane_steps = sorted(
        ((dy, dx) for dy in range(ny) for dx in range(nx) if (dy, dx) != (0, 0)),
        key=lambda step: -min(step[0], ny - step[0]) - min(step[1], nx - step[1]),
    )
    row, col = lax.axis_index("row"), lax.axis_index("col")
    y, x = lax.div(row, nx), lax.rem(row, nx)
    z, core = lax.div(col, 2), lax.rem(col, 2)
    parity, slot = lax.rem(row, 2), lax.div(row, 2)
    holder = parity == core
    sibling = 2 * z + 1 - core

    def beside(step):
        return lax.rem(y + step[0], ny) * nx + lax.rem(x + step[1], nx)

    def send(source, target, send_sem, recv_sem, to_row, to_col):
        copy = pltpu.make_async_remote_copy(
            src_ref=source, dst_ref=target, send_sem=send_sem, recv_sem=recv_sem,
            device_id={"row": to_row, "col": to_col}, device_id_type=MESH,
        )
        copy.start()

    def arrive(place, recv_sem):
        pltpu.make_async_remote_copy(
            src_ref=place, dst_ref=place, send_sem=s_swap.at[0], recv_sem=recv_sem,
            device_id={"row": row, "col": sibling}, device_id_type=MESH,
        ).wait_recv()

    def sent(place, send_sem):
        pltpu.make_async_remote_copy(
            src_ref=place, dst_ref=place, send_sem=send_sem, recv_sem=r_swap.at[0],
            device_id={"row": row, "col": sibling}, device_id_type=MESH,
        ).wait_send()

    own_copies = [
        pltpu.make_async_copy(diag_hbm, diag.at[core], local_sem.at[0]),
        pltpu.make_async_copy(cross_hbm, cross.at[core], local_sem.at[1]),
        pltpu.make_async_copy(loads_hbm.at[0], loads.at[core], local_sem.at[2]),
        pltpu.make_async_copy(rest_hbm, rest, local_sem.at[3]),
        pltpu.make_async_copy(
            coupling_hbm.at[:, :, pl.ds(pl.multiple_of(x * qx, qx), qx)], raw_x.at[core, :, x], local_sem.at[4]
        ),
        pltpu.make_async_copy(
            coupling_hbm.at[:, :, pl.ds(pl.multiple_of(nx * qx + y * qy, qy), qy)], raw_y.at[core, :, y], local_sem.at[5]
        ),
    ]
    for copy in own_copies:
        copy.start()
    own_upper = [
        pltpu.make_async_copy(loads_hbm.at[1, pl.ds(h * part, part)], gathered.at[h, slot, core], local_sem.at[6 + h])
        for h in (0, 1)
    ]

    @pl.when(holder)
    def _():
        for copy in own_upper:
            copy.start()

    barrier = pltpu.get_barrier_semaphore()

    @pl.loop(0, rows)
    def _(step):
        peer = lax.rem(row + step, rows)
        pl.semaphore_signal(barrier, inc=1, device_id={"row": peer, "col": sibling}, device_id_type=MESH)

        @pl.when(step > 0)
        def _():
            pl.semaphore_signal(barrier, inc=1, device_id={"row": peer, "col": col}, device_id_type=MESH)

    @pl.loop(1, nz)
    def _(step):
        peer = lax.rem(z + step, nz)
        pl.semaphore_signal(barrier, inc=1, device_id={"row": row, "col": 2 * peer + core}, device_id_type=MESH)

    pl.semaphore_wait(barrier, 2 * rows - 1 + nz - 1)

    def rows_of(h):
        return pl.ds(h * part, part)

    def scatter_z(h, parts, landing, s_sem, r_sem):
        for step in z_steps:
            peer = lax.rem(z + step, nz)
            send(parts.at[h, peer], landing.at[h, z], s_sem.at[h, peer], r_sem.at[h, z], row, 2 * peer + core)

    def total_z(h, parts, landing, r_sem):
        value = parts[h, z]
        for step in z_steps:
            peer = lax.rem(z + step, nz)
            arrive(landing.at[h, peer], r_sem.at[h, peer])
            value = value + landing[h, peer]
        return value

    def spread_z(h, panel, value, s_sem, r_sem):
        place = solved.at[panel, z, core, rows_of(h)]
        place[...] = value
        for step in z_steps:
            peer = lax.rem(z + step, nz)
            send(place, place, s_sem.at[h, peer], r_sem.at[h, z], row, 2 * peer + core)

    def found_z(h, panel, r_sem):
        for step in z_steps:
            peer = lax.rem(z + step, nz)
            arrive(solved.at[panel, peer, core, rows_of(h)], r_sem.at[h, peer])
        found = solved[panel, :, core, rows_of(h)]
        along_x[panel, x, :, rows_of(h)] = found
        along_y[panel, y, :, rows_of(h)] = found
        return found.reshape(nz * part, width)

    def gather_upper(h):
        source = loads_hbm.at[1, rows_of(h)]
        target = gathered.at[h, slot, core]
        for step in plane_steps:
            peer = beside(step)
            send(source, target, s_a.at[h, peer], r_a.at[h, slot, core], peer, 2 * z + parity)

        @pl.when(jnp.logical_not(holder))
        def _():
            send(source, target, s_a.at[h, row], r_a.at[h, slot, core], row, sibling)

    def multiply_upper(h):
        for block in range(nz):
            for source in (0, 1):
                @pl.when(jnp.logical_not(jnp.logical_and(2 * block + core == row, source == core)))
                def _():
                    arrive(gathered.at[h, block, source], r_a.at[h, block, source])
        left = jnp.concatenate([gathered[h, :, source].reshape(nz * part, width) for source in (0, 1)], axis=1)
        part_up[h] = product(halves(left), upper_diag).reshape(nz, part, width)
        scatter_z(h, part_up, land_up, s_b, r_b)

    def multiply_cross(h):
        upper = found_z(h, 1, r_c)
        part_cross[h] = product(halves(upper), cross_halves).reshape(nz, part, 2 * width)
        for step in range(nz):
            block = lax.rem(slot + nz // 2 + step, nz)
            owner = 2 * block + core

            @pl.when(owner != row)
            def _():
                send(part_cross.at[h, block], land_cross.at[h, row], s_d.at[h, block], r_d.at[h, row], owner, col)

    def reduce_cross(h):
        @pl.when(holder)
        def _():
            value = jnp.concatenate([loads[0, rows_of(h)], loads[1, rows_of(h)]], axis=1) - part_cross[h, slot]
            for step in plane_steps:
                peer = beside(step)
                arrive(land_cross.at[h, peer], r_d.at[h, peer])
                value = value - land_cross[h, peer]
            place = lower.at[h, slot]
            place[...] = value
            for step in plane_steps:
                peer = beside(step)
                send(place, place, s_e.at[h, peer], r_e.at[h, slot], peer, col)

    def multiply_lower(h):
        for block in range(nz):
            @pl.when(2 * block + core != row)
            def _():
                arrive(lower.at[h, block], r_e.at[h, block])
        part_low[h] = product(halves(lower[h].reshape(nz * part, 2 * width)), lower_diag).reshape(nz, part, width)
        scatter_z(h, part_low, land_low, s_f, r_f)

    def forward(h, panel):
        for step in x_steps:
            peer = lax.rem(x + step, nx)
            place = along_x.at[panel, x, :, rows_of(h)]
            send(place, place, s_lx.at[h, panel, peer], r_lx.at[h, panel, x], y * nx + peer, col)
        for step in y_steps:
            peer = lax.rem(y + step, ny)
            place = along_y.at[panel, y, :, rows_of(h)]
            send(place, place, s_ly.at[h, panel, peer], r_ly.at[h, panel, y], peer * nx + x, col)

    def deal(panel):
        for step in x_steps:
            peer = lax.rem(x + step, nx)
            send(
                coupling_hbm.at[panel, :, pl.ds(pl.multiple_of(peer * qx, qx), qx)], raw_x.at[core, panel, x],
                s_px.at[panel, peer], r_px.at[panel, x], y * nx + peer, col,
            )
        for step in y_steps:
            peer = lax.rem(y + step, ny)
            send(
                coupling_hbm.at[panel, :, pl.ds(pl.multiple_of(nx * qx + peer * qy, qy), qy)], raw_y.at[core, panel, y],
                s_py.at[panel, peer], r_py.at[panel, y], peer * nx + x, col,
            )

    def share_dealt(panel):
        for step in x_steps:
            peer = lax.rem(x + step, nx)
            arrive(raw_x.at[core, panel, peer], r_px.at[panel, peer])
        send(raw_x.at[core, panel], raw_x.at[core, panel], s_deal.at[panel, 0], r_deal.at[panel, 0], row, sibling)
        for step in y_steps:
            peer = lax.rem(y + step, ny)
            arrive(raw_y.at[core, panel, peer], r_py.at[panel, peer])
        send(raw_y.at[core, panel], raw_y.at[core, panel], s_deal.at[panel, 1], r_deal.at[panel, 1], row, sibling)

    def split_dealt(panel):
        arrive(raw_x.at[1 - core, panel], r_deal.at[panel, 0])
        arrive(raw_y.at[1 - core, panel], r_deal.at[panel, 1])
        for raw, high, low, groups in ((raw_x, high_x, low_x, nx), (raw_y, high_y, low_y, ny)):
            @pl.loop(0, 2 * groups)
            def _(index):
                owner, group = lax.div(index, groups), lax.rem(index, groups)
                start = pl.multiple_of((panel * groups + group) * width, width)
                block_high, block_low = halves(raw[owner, panel, group])
                high[owner, pl.ds(start, width)] = block_high
                low[owner, pl.ds(start, width)] = block_low

    send(diag_hbm, diag.at[core], s_swap.at[0], r_swap.at[0], row, sibling)
    gather_upper(0)
    gather_upper(1)
    send(cross_hbm, cross.at[core], s_swap.at[1], r_swap.at[1], row, sibling)
    send(loads_hbm.at[0], loads.at[core], s_swap.at[2], r_swap.at[2], row, sibling)

    own_copies[0].wait()
    arrive(diag.at[1 - core], r_swap.at[0])

    @pl.when(holder)
    def _():
        for copy in own_upper:
            copy.wait()

    upper_diag = halves(diag[:, 1].reshape(2 * width, width))
    multiply_upper(0)
    deal(1)
    multiply_upper(1)

    own_copies[1].wait()
    arrive(cross.at[1 - core], r_swap.at[1])
    cross_halves = halves(jnp.concatenate([cross[0], cross[1]], axis=1))
    for h in (0, 1):
        spread_z(h, 1, total_z(h, part_up, land_up, r_b), s_c, r_c)

    own_copies[2].wait()
    arrive(loads.at[1 - core], r_swap.at[2])
    for h in (0, 1):
        multiply_cross(h)
    for h in (0, 1):
        reduce_cross(h)
    deal(0)

    lower_diag = halves(diag[:, 0].reshape(2 * width, width))
    for h in (0, 1):
        multiply_lower(h)

    for h in (0, 1):
        forward(h, 1)
    send(solved.at[1, :, core], solved.at[1, :, core], s_out.at[1], r_out.at[1], row, sibling)

    own_copies[4].wait()
    own_copies[5].wait()
    for h in (0, 1):
        spread_z(h, 0, total_z(h, part_low, land_low, r_f), s_g, r_g)
    share_dealt(1)
    share_dealt(0)
    for h in (0, 1):
        found_z(h, 0, r_g)
        forward(h, 0)
    send(solved.at[0, :, core], solved.at[0, :, core], s_out.at[0], r_out.at[0], row, sibling)
    split_dealt(1)
    split_dealt(0)

    for h in (0, 1):
        for panel in (1, 0):
            for step in x_steps:
                peer = lax.rem(x + step, nx)
                arrive(along_x.at[panel, peer, :, rows_of(h)], r_lx.at[h, panel, peer])
            for step in y_steps:
                peer = lax.rem(y + step, ny)
                arrive(along_y.at[panel, peer, :, rows_of(h)], r_ly.at[h, panel, peer])

    def tile_over_y(peer):
        start = peer * half
        left = halves(jnp.concatenate(
            [along_x[panel, group, pl.ds(start, half)].reshape(half * height, width) for panel in (0, 1) for group in range(nx)],
            axis=1,
        ))
        for owner in (0, 1):
            value = product(left, (high_x[owner], low_x[owner]))
            sum_x[peer, :, owner] = value.reshape(half, height, qx)

        @pl.when(peer != y)
        def _():
            send(sum_x.at[peer], land_x.at[y], s_sx.at[peer], r_sx.at[y], peer * nx + x, col)

    def tile_over_x(offset):
        for start in range(0, ny, half):
            left = halves(jnp.concatenate(
                [
                    jnp.concatenate([along_y[panel, group, (start + part) * half + offset] for part in range(half)], axis=0)
                    for panel in (0, 1) for group in range(ny)
                ],
                axis=1,
            ))
            for owner in (0, 1):
                value = product(left, (high_y[owner], low_y[owner]))
                sum_y[offset, pl.ds(start, half), owner] = value.reshape(half, height, qy)
        target = 2 * offset + core

        @pl.when(target != x)
        def _():
            send(sum_y.at[offset], land_y.at[x], s_sy.at[offset], r_sy.at[x], y * nx + target, col)

    @pl.loop(0, half)
    def _(step):
        tile_over_y(lax.rem(y + half - step, ny))
        tile_over_x(lax.rem(lax.div(x, 2) + 1 + step, half))
        tile_over_y(lax.rem(y + (half + 1) * (1 - step), ny))

    own_copies[3].wait()

    @pl.loop(1, ny)
    def _(step):
        peer = lax.rem(y + step, ny)
        arrive(land_x.at[peer], r_sx.at[peer])

    for offset in range(half):
        for owner in (0, 1):
            value = sum_x[y, offset, owner]
            for distance in range(1, ny):
                value = value + land_x[lax.rem(y + distance, ny), offset, owner]
            target = 2 * offset + core
            here = jnp.logical_and(target == x, owner == core)
            done_x[offset, owner] = value

            @pl.when(jnp.logical_not(here))
            def _():
                send(
                    done_x.at[offset, owner], tile_x.at[x], s_tx.at[offset, owner], r_tx.at[x],
                    y * nx + target, 2 * z + owner,
                )

    @pl.when(holder)
    def _():
        @pl.loop(1, nx)
        def _(step):
            peer = lax.rem(x + step, nx)
            arrive(land_y.at[peer], r_sy.at[peer])

        for peer in range(ny):
            for owner in (0, 1):
                value = sum_y[lax.div(x, 2), peer, owner]
                for distance in range(1, nx):
                    value = value + land_y[lax.rem(x + distance, nx), peer, owner]
                done_y[peer, owner] = value

                @pl.when(jnp.logical_not(jnp.logical_and(peer == y, owner == core)))
                def _():
                    send(
                        done_y.at[peer, owner], tile_y.at[y], s_ty.at[peer, owner], r_ty.at[y],
                        peer * nx + x, 2 * z + owner,
                    )

        tile_x[x] = done_x[lax.div(x, 2), core]
        tile_y[y] = done_y[y, core]

    for group in range(nx):
        @pl.when(jnp.logical_not(jnp.logical_and(holder, group == x)))
        def _():
            arrive(tile_x.at[group], r_tx.at[group])

        columns = pl.ds(group * qx, qx)
        out[:, columns] = rest[:, columns] - tile_x[group]

    for group in range(ny):
        @pl.when(jnp.logical_not(jnp.logical_and(holder, group == y)))
        def _():
            arrive(tile_y.at[group], r_ty.at[group])

        columns = pl.ds(nx * qx + group * qy, qy)
        out[:, columns] = rest[:, columns] - tile_y[group]

    for panel in (0, 1):
        arrive(solved.at[panel, :, 1 - core], r_out.at[panel])

    sent(diag.at[core], s_swap.at[0])
    sent(cross.at[core], s_swap.at[1])
    sent(loads.at[core], s_swap.at[2])
    for panel in (0, 1):
        sent(solved.at[panel, :, core], s_out.at[panel])
    for panel in (0, 1):
        sent(raw_x.at[core, panel], s_deal.at[panel, 0])
        sent(raw_y.at[core, panel], s_deal.at[panel, 1])

    for h in (0, 1):
        @pl.loop(0, rows)
        def _(step):
            peer = lax.rem(row + step, rows)

            @pl.when(jnp.logical_or(step > 0, jnp.logical_not(holder)))
            def _():
                sent(gathered.at[0, 0, 0], s_a.at[h, peer])

            @pl.when(jnp.logical_and(step > 0, holder))
            def _():
                sent(lower.at[0, 0], s_e.at[h, peer])

        @pl.loop(1, nz)
        def _(step):
            peer = lax.rem(z + step, nz)
            for sem in (s_b, s_c, s_f, s_g):
                sent(part_up.at[0, 0], sem.at[h, peer])

        @pl.loop(0, nz)
        def _(block):
            @pl.when(2 * block + core != row)
            def _():
                sent(part_cross.at[0, 0], s_d.at[h, block])

        for panel in (0, 1):
            for step in x_steps:
                sent(along_x.at[0, 0, :, rows_of(0)], s_lx.at[h, panel, lax.rem(x + step, nx)])
            for step in y_steps:
                sent(along_y.at[0, 0, :, rows_of(0)], s_ly.at[h, panel, lax.rem(y + step, ny)])

    @pl.loop(1, nx)
    def _(step):
        peer = lax.rem(x + step, nx)
        for panel in (0, 1):
            sent(raw_x.at[core, panel, 0], s_px.at[panel, peer])

    @pl.loop(1, ny)
    def _(step):
        peer = lax.rem(y + step, ny)
        for panel in (0, 1):
            sent(raw_y.at[core, panel, 0], s_py.at[panel, peer])
        sent(sum_x.at[0], s_sx.at[peer])

    @pl.loop(0, half)
    def _(offset):
        target = 2 * offset + core

        @pl.when(target != x)
        def _():
            sent(sum_y.at[0], s_sy.at[offset])

        for owner in (0, 1):
            @pl.when(jnp.logical_not(jnp.logical_and(target == x, owner == core)))
            def _():
                sent(done_x.at[0, 0], s_tx.at[offset, owner])

    @pl.when(holder)
    def _():
        @pl.loop(0, ny)
        def _(peer):
            for owner in (0, 1):
                @pl.when(jnp.logical_not(jnp.logical_and(peer == y, owner == core)))
                def _():
                    sent(done_y.at[0, 0], s_ty.at[peer, owner])


def local(mesh, diag_inv, cross_block, coupling, panel_loads, rest_loads):
    rows, cols = mesh.shape["row"], mesh.shape["col"]
    nx = ny = math.isqrt(rows)
    nz, half = cols // 2, math.isqrt(rows) // 2
    _, height, width = panel_loads.shape
    span = rest_loads.shape[1]
    qx, qy = span // 2 // nx, span // 2 // ny
    f32, bf16 = jnp.float32, jnp.bfloat16
    vmem, dma = pltpu.VMEM, lambda *shape: pltpu.SemaphoreType.DMA(shape)
    block, piece = (height, width), (height // 2, width)
    whole = pl.BlockSpec(memory_space=pltpu.VMEM)
    solved, rest_updated = pl.pallas_call(
        functools.partial(solve_kernel, (rows, nx, ny, nz, height, width, qx, qy)),
        out_shape=(
            jax.ShapeDtypeStruct((2, nz, 2) + block, f32),
            jax.ShapeDtypeStruct((height, span), f32),
        ),
        in_specs=[pl.BlockSpec(memory_space=pltpu.HBM)] * 5,
        out_specs=(whole, whole),
        scratch_shapes=[
            vmem((2, 2, width, width), f32),
            vmem((2, width, width), f32),
            vmem((2,) + block, f32),
            vmem((height, span), f32),
            vmem((2, nz, 2) + piece, f32),
            vmem((2, nz) + piece, f32),
            vmem((2, nz) + piece, f32),
            vmem((2, nz, height // 2, 2 * width), f32),
            vmem((2, rows, height // 2, 2 * width), f32),
            vmem((2, nz, height // 2, 2 * width), f32),
            vmem((2, nz) + piece, f32),
            vmem((2, nz) + piece, f32),
            vmem((2, 2, nx, width, qx), f32),
            vmem((2, 2, ny, width, qy), f32),
            vmem((2, 2 * nx * width, qx), bf16),
            vmem((2, 2 * nx * width, qx), bf16),
            vmem((2, 2 * ny * width, qy), bf16),
            vmem((2, 2 * ny * width, qy), bf16),
            vmem((2, nx, nz) + block, f32),
            vmem((2, ny, nz) + block, f32),
            vmem((ny, half, 2, height, qx), f32),
            vmem((ny, half, 2, height, qx), f32),
            vmem((half, ny, 2, height, qy), f32),
            vmem((nx, ny, 2, height, qy), f32),
            vmem((half, 2, height, qx), f32),
            vmem((ny, 2, height, qy), f32),
            vmem((nx, height, qx), f32),
            vmem((ny, height, qy), f32),
            dma(8), dma(3), dma(3),
            dma(2, rows), dma(2, nz, 2),
            dma(2, nz), dma(2, nz), dma(2, nz), dma(2, nz),
            dma(2, nz), dma(2, rows), dma(2, rows), dma(2, nz),
            dma(2, nz), dma(2, nz), dma(2, nz), dma(2, nz),
            dma(2, nx), dma(2, nx), dma(2, ny), dma(2, ny), dma(2, 2), dma(2, 2),
            dma(2, 2, nx), dma(2, 2, nx), dma(2, 2, ny), dma(2, 2, ny),
            dma(ny), dma(ny), dma(half), dma(nx),
            dma(half, 2), dma(nx), dma(ny, 2), dma(ny),
            dma(2), dma(2),
        ],
        compiler_params=pltpu.CompilerParams(
            collective_id=0, has_side_effects=True, vmem_limit_bytes=42 * 2**20
        ),
    )(*(pltpu.with_memory_space_constraint(arg, pltpu.HBM) for arg in (diag_inv, cross_block, coupling, panel_loads, rest_loads)))
    return solved.reshape(2, rows * height, width), rest_updated


def solution(mesh):
    in_specs = (
        P(None, "col", "row"),
        P("row", "col"),
        P(None, "row", "col"),
        P(None, "row", "col"),
        P("row", "col"),
    )
    out_specs = (P(None, None, "row"), P("row", "col"))
    return jax.shard_map(
        functools.partial(local, mesh), mesh=mesh, in_specs=in_specs, out_specs=out_specs, check_vma=False
    )
```

time: 133 us -> 123 us (0.925)
  Pallas kernels: 128 us -> 119 us
  local copies, waits for them, and re-layouts: 4.53 us -> 1.94 us
    pallas_call x1, Pallas kernels: 128 us -> 119 us  [local(): pl.pallas_call(functools.partial(solve_kernel, (rows, nx, ny, nz, height,...]
    unnamed x2, local copies, waits for them, and re-layouts: 4.53 us -> 1.94 us
where the time goes in v3:
time: 123 us; the launch traced here: 122 us
  Pallas kernels  119 us (97%)
  local copies, waits for them, and re-layouts  1.94 us (2%)
    pallas_call x1, Pallas kernels, local(): pl.pallas_call(functools.partial(solve_kernel, (rows, nx, ny, nz, height,...  119 us

profile of v3, /device:TPU:1, one launch (start us, length us, event | category | flops | bytes accessed | tf_op | source)
XLA Modules:
  0.0 122.0 jit_solution(16023622055030877724)
XLA Ops:
  0.6 119.5 %shard_map.68 = (f32[2,8,2,64,128]{4,3,2,1,0:T(8,128)S(1)}, f32[64,4096]{1,0:T(8,128)S(1)}) custom-call(f32[2,128,128]{2,1,0:T(8,128)} %diag_hbm.1, f32[128,128]{1,0:T(8,128)} %cross_hbm.1, f32[2,128,4096]{2,1,0:T(8,128)} %coupling_hbm.1, f32[2,64,128]{2,1,0:T(8,128)} %loads_hbm.1, f32[64,4096]{1,0:T(8,128)} %rest_hbm.1), custom_call_target="tpu_custom_call" | custom-call | tf_op jit(solution)/shard_map/pallas_call | solution.py:507
  120.1 1.0 copy.9
  121.1 1.0 copy.10

commit v4 on v3

--- a/solution.py
+++ b/solution.py
@@ -35,10 +35,10 @@
     diag, cross, loads, rest,
     gathered, part_up, land_up, part_cross, land_cross, lower, part_low, land_low,
     raw_x, raw_y, high_x, low_x, high_y, low_y,
-    along_x, along_y, sum_x, land_x, sum_y, land_y, done_x, done_y, tile_x, tile_y,
+    along_x, along_y, sum_x, land_x, relay_x, sum_y, land_y, relay_y, done_x, done_y, tile_x, tile_y,
     local_sem, s_swap, r_swap, s_a, r_a, s_b, r_b, s_c, r_c, s_d, r_d, s_e, r_e, s_f, r_f, s_g, r_g,
     s_px, r_px, s_py, r_py, s_deal, r_deal, s_lx, r_lx, s_ly, r_ly,
-    s_sx, r_sx, s_sy, r_sy, s_tx, r_tx, s_ty, r_ty, s_out, r_out,
+    s_sx, r_sx, s_sy, r_sy, s_rx, r_rx, s_ry, r_ry, s_far, r_far, s_fz, r_fz, s_tx, r_tx, s_ty, r_ty, s_out, r_out,
 ):
     rows, nx, ny, nz, height, width, qx, qy = dims
     half, part = nx // 2, height // 2
@@ -205,11 +205,11 @@
         scatter_z(h, part_low, land_low, s_f, r_f)
 
     def forward(h, panel):
-        for step in x_steps:
+        for step in x_steps[panel:]:
             peer = lax.rem(x + step, nx)
             place = along_x.at[panel, x, :, rows_of(h)]
             send(place, place, s_lx.at[h, panel, peer], r_lx.at[h, panel, x], y * nx + peer, col)
-        for step in y_steps:
+        for step in y_steps[panel:]:
             peer = lax.rem(y + step, ny)
             place = along_y.at[panel, y, :, rows_of(h)]
             send(place, place, s_ly.at[h, panel, peer], r_ly.at[h, panel, y], peer * nx + x, col)
@@ -275,10 +275,22 @@
     for h in (0, 1):
         spread_z(h, 1, total_z(h, part_up, land_up, r_b), s_c, r_c)
 
+    x_far, y_far = lax.rem(x + half, nx), lax.rem(y + half, ny)
+    own_block = solved.at[1, z, core]
+    send(own_block, along_x.at[1, x, z], s_far.at[0], r_far.at[0], y * nx + x_far, col)
+    send(own_block, along_y.at[1, y, z], s_far.at[1], r_far.at[1], y_far * nx + x, col)
+
     own_copies[2].wait()
     arrive(loads.at[1 - core], r_swap.at[2])
     for h in (0, 1):
         multiply_cross(h)
+    far_places = (along_x.at[1, x_far], along_y.at[1, y_far])
+    for axis in (0, 1):
+        place = far_places[axis].at[z]
+        arrive(place, r_far.at[axis])
+        for step in z_steps:
+            peer = lax.rem(z + step, nz)
+            send(place, place, s_fz.at[axis, peer], r_fz.at[axis, z], row, 2 * peer + core)
     for h in (0, 1):
         reduce_cross(h)
     deal(0)
@@ -306,12 +318,17 @@
 
     for h in (0, 1):
         for panel in (1, 0):
-            for step in x_steps:
+            for step in x_steps[panel:]:
                 peer = lax.rem(x + step, nx)
                 arrive(along_x.at[panel, peer, :, rows_of(h)], r_lx.at[h, panel, peer])
-            for step in y_steps:
+            for step in y_steps[panel:]:
                 peer = lax.rem(y + step, ny)
                 arrive(along_y.at[panel, peer, :, rows_of(h)], r_ly.at[h, panel, peer])
+
+    for axis in (0, 1):
+        for step in z_steps:
+            peer = lax.rem(z + step, nz)
+            arrive(far_places[axis].at[peer], r_fz.at[axis, peer])
 
     def tile_over_y(peer):
         start = peer * half
@@ -322,10 +339,6 @@
         for owner in (0, 1):
             value = product(left, (high_x[owner], low_x[owner]))
             sum_x[peer, :, owner] = value.reshape(half, height, qx)
-
-        @pl.when(peer != y)
-        def _():
-            send(sum_x.at[peer], land_x.at[y], s_sx.at[peer], r_sx.at[y], peer * nx + x, col)
 
     def tile_over_x(offset):
         for start in range(0, ny, half):
@@ -339,30 +352,75 @@
             for owner in (0, 1):
                 value = product(left, (high_y[owner], low_y[owner]))
                 sum_y[offset, pl.ds(start, half), owner] = value.reshape(half, height, qy)
-        target = 2 * offset + core
-
-        @pl.when(target != x)
-        def _():
-            send(sum_y.at[offset], land_y.at[x], s_sy.at[offset], r_sy.at[x], y * nx + target, col)
-
-    @pl.loop(0, half)
+    y_up, y_down = lax.rem(y + 1, ny), lax.rem(y + ny - 1, ny)
+    x_up, x_down = lax.rem(x + 1, nx), lax.rem(x + nx - 1, nx)
+    row_up, row_down = y_up * nx + x, y_down * nx + x
+    side_up, side_down = y * nx + x_up, y * nx + x_down
+    own_offset = lax.div(x, 2)
+    up_offset, down_offset = lax.div(x_up, 2), lax.div(x_down, 2)
+    first, last = pl.ds(0, half), pl.ds(half, half)
+
+    @pl.loop(0, 2)
     def _(step):
-        tile_over_y(lax.rem(y + half - step, ny))
-        tile_over_x(lax.rem(lax.div(x, 2) + 1 + step, half))
-        tile_over_y(lax.rem(y + (half + 1) * (1 - step), ny))
+        tile_over_y(jnp.where(step == 0, y_far, y_down))
+
+        @pl.when(step == 0)
+        def _():
+            send(sum_x.at[y_far, 0], relay_x.at[0], s_rx.at[0], r_rx.at[0], row_up, col)
+            send(sum_x.at[y_far, 1], relay_x.at[1], s_rx.at[1], r_rx.at[1], row_down, col)
+
+        @pl.when(step == 1)
+        def _():
+            send(sum_x.at[y_down, 0], land_x.at[1, 0], s_sx.at[1, 0], r_sx.at[1, 0], row_down, col)
+
+        tile_over_x(jnp.where(
+            step == 0, jnp.where(holder, 1 - own_offset, up_offset), jnp.where(holder, own_offset, down_offset)
+        ))
+
+        @pl.when(jnp.logical_and(step == 0, holder))
+        def _():
+            send(sum_y.at[1 - own_offset, first], relay_y.at[0], s_ry.at[0], r_ry.at[0], side_up, col)
+            send(sum_y.at[1 - own_offset, last], relay_y.at[1], s_ry.at[1], r_ry.at[1], side_down, col)
+
+        @pl.when(jnp.logical_and(step == 0, jnp.logical_not(holder)))
+        def _():
+            send(sum_y.at[up_offset, last], land_y.at[0, last], s_sy.at[0, 1], r_sy.at[0, 1], side_up, col)
+
+        @pl.when(jnp.logical_and(step == 1, jnp.logical_not(holder)))
+        def _():
+            send(sum_y.at[down_offset, first], land_y.at[1, first], s_sy.at[1, 0], r_sy.at[1, 0], side_down, col)
+
+        @pl.when(step == 1)
+        def _():
+            arrive(relay_x.at[0], r_rx.at[0])
+            sum_x[y_up, 0] = sum_x[y_up, 0] + relay_x[0]
+            send(sum_x.at[y_up, 0], land_x.at[0, 0], s_sx.at[0, 0], r_sx.at[0, 0], row_up, col)
+            arrive(relay_x.at[1], r_rx.at[1])
+            sum_x[y_down, 1] = sum_x[y_down, 1] + relay_x[1]
+            send(sum_x.at[y_down, 1], land_x.at[1, 1], s_sx.at[1, 1], r_sx.at[1, 1], row_down, col)
+
+            @pl.when(jnp.logical_not(holder))
+            def _():
+                arrive(relay_y.at[0], r_ry.at[0])
+                sum_y[up_offset, first] = sum_y[up_offset, first] + relay_y[0]
+                send(sum_y.at[up_offset, first], land_y.at[0, first], s_sy.at[0, 0], r_sy.at[0, 0], side_up, col)
+                arrive(relay_y.at[1], r_ry.at[1])
+                sum_y[down_offset, last] = sum_y[down_offset, last] + relay_y[1]
+                send(sum_y.at[down_offset, last], land_y.at[1, last], s_sy.at[1, 1], r_sy.at[1, 1], side_down, col)
+
+        tile_over_y(jnp.where(step == 0, y_up, y))
+
+        @pl.when(step == 0)
+        def _():
+            send(sum_x.at[y_up, 1], land_x.at[0, 1], s_sx.at[0, 1], r_sx.at[0, 1], row_up, col)
 
     own_copies[3].wait()
 
-    @pl.loop(1, ny)
-    def _(step):
-        peer = lax.rem(y + step, ny)
-        arrive(land_x.at[peer], r_sx.at[peer])
-
     for offset in range(half):
+        for side in (0, 1):
+            arrive(land_x.at[side, offset], r_sx.at[side, offset])
         for owner in (0, 1):
-            value = sum_x[y, offset, owner]
-            for distance in range(1, ny):
-                value = value + land_x[lax.rem(y + distance, ny), offset, owner]
+            value = sum_x[y, offset, owner] + land_x[0, offset, owner] + land_x[1, offset, owner]
             target = 2 * offset + core
             here = jnp.logical_and(target == x, owner == core)
             done_x[offset, owner] = value
@@ -376,16 +434,12 @@
 
     @pl.when(holder)
     def _():
-        @pl.loop(1, nx)
-        def _(step):
-            peer = lax.rem(x + step, nx)
-            arrive(land_y.at[peer], r_sy.at[peer])
-
         for peer in range(ny):
+            if peer % half == 0:
+                for side in (0, 1):
+                    arrive(land_y.at[side, pl.ds(peer, half)], r_sy.at[side, peer // half])
             for owner in (0, 1):
-                value = sum_y[lax.div(x, 2), peer, owner]
-                for distance in range(1, nx):
-                    value = value + land_y[lax.rem(x + distance, nx), peer, owner]
+                value = sum_y[own_offset, peer, owner] + land_y[0, peer, owner] + land_y[1, peer, owner]
                 done_y[peer, owner] = value
 
                 @pl.when(jnp.logical_not(jnp.logical_and(peer == y, owner == core)))
@@ -452,9 +506,9 @@
                 sent(part_cross.at[0, 0], s_d.at[h, block])
 
         for panel in (0, 1):
-            for step in x_steps:
+            for step in x_steps[panel:]:
                 sent(along_x.at[0, 0, :, rows_of(0)], s_lx.at[h, panel, lax.rem(x + step, nx)])
-            for step in y_steps:
+            for step in y_steps[panel:]:
                 sent(along_y.at[0, 0, :, rows_of(0)], s_ly.at[h, panel, lax.rem(y + step, ny)])
 
     @pl.loop(1, nx)
@@ -468,20 +522,32 @@
         peer = lax.rem(y + step, ny)
         for panel in (0, 1):
             sent(raw_y.at[core, panel, 0], s_py.at[panel, peer])
-        sent(sum_x.at[0], s_sx.at[peer])
 
     @pl.loop(0, half)
     def _(offset):
         target = 2 * offset + core
-
-        @pl.when(target != x)
-        def _():
-            sent(sum_y.at[0], s_sy.at[offset])
-
         for owner in (0, 1):
             @pl.when(jnp.logical_not(jnp.logical_and(target == x, owner == core)))
             def _():
                 sent(done_x.at[0, 0], s_tx.at[offset, owner])
+
+    for axis in (0, 1):
+        sent(own_block, s_far.at[axis])
+        for step in z_steps:
+            sent(own_block, s_fz.at[axis, lax.rem(z + step, nz)])
+
+    for side in (0, 1):
+        sent(relay_x.at[0], s_rx.at[side])
+        for piece in (0, 1):
+            sent(land_x.at[0, 0], s_sx.at[side, piece])
+
+            @pl.when(jnp.logical_not(holder))
+            def _():
+                sent(land_y.at[0, first], s_sy.at[side, piece])
+
+        @pl.when(holder)
+        def _():
+            sent(relay_y.at[0], s_ry.at[side])
 
     @pl.when(holder)
     def _():
@@ -534,9 +600,11 @@
             vmem((2, nx, nz) + block, f32),
             vmem((2, ny, nz) + block, f32),
             vmem((ny, half, 2, height, qx), f32),
-            vmem((ny, half, 2, height, qx), f32),
+            vmem((2, half, 2, height, qx), f32),
+            vmem((2, 2, height, qx), f32),
             vmem((half, ny, 2, height, qy), f32),
-            vmem((nx, ny, 2, height, qy), f32),
+            vmem((2, ny, 2, height, qy), f32),
+            vmem((2, half, 2, height, qy), f32),
             vmem((half, 2, height, qx), f32),
             vmem((ny, 2, height, qy), f32),
             vmem((nx, height, qx), f32),
@@ -548,7 +616,8 @@
             dma(2, nz), dma(2, nz), dma(2, nz), dma(2, nz),
             dma(2, nx), dma(2, nx), dma(2, ny), dma(2, ny), dma(2, 2), dma(2, 2),
             dma(2, 2, nx), dma(2, 2, nx), dma(2, 2, ny), dma(2, 2, ny),
-            dma(ny), dma(ny), dma(half), dma(nx),
+            dma(2, 2), dma(2, 2), dma(2, 2), dma(2, 2), dma(2), dma(2), dma(2), dma(2),
+            dma(2), dma(2), dma(2, nz), dma(2, nz),
             dma(half, 2), dma(nx), dma(ny, 2), dma(ny),
             dma(2), dma(2),
         ],

time: 123 us -> 116 us (0.943)
  Pallas kernels: 119 us -> 112 us
    pallas_call x1, Pallas kernels: 119 us -> 112 us  [local(): pl.pallas_call(functools.partial(solve_kernel, (rows, nx, ny, nz, height,...]
where the time goes in v4:
time: 116 us; the launch traced here: 115 us
  Pallas kernels  112 us (97%)
  local copies, waits for them, and re-layouts  1.94 us (2%)
    pallas_call x1, Pallas kernels, local(): pl.pallas_call(functools.partial(solve_kernel, (rows, nx, ny, nz, height,...  112 us

profile of v4, /device:TPU:1, one launch (start us, length us, event | category | flops | bytes accessed | tf_op | source)
XLA Modules:
  0.0 114.9 jit_solution(1997323911804619830)
XLA Ops:
  0.6 112.4 %shard_map.68 = (f32[2,8,2,64,128]{4,3,2,1,0:T(8,128)S(1)}, f32[64,4096]{1,0:T(8,128)S(1)}) custom-call(f32[2,128,128]{2,1,0:T(8,128)} %diag_hbm.1, f32[128,128]{1,0:T(8,128)} %cross_hbm.1, f32[2,128,4096]{2,1,0:T(8,128)} %coupling_hbm.1, f32[2,64,128]{2,1,0:T(8,128)} %loads_hbm.1, f32[64,4096]{1,0:T(8,128)} %rest_hbm.1), custom_call_target="tpu_custom_call" | custom-call | tf_op jit(solution)/shard_map/pallas_call | solution.py:573
  113.0 1.0 copy.9
  114.0 1.0 copy.10

commit v5 on v4

--- a/solution.py
+++ b/solution.py
@@ -21,7 +21,9 @@
     left_high, left_low = left_halves
     right_high, right_low = right_halves
     dot = functools.partial(jnp.dot, preferred_element_type=jnp.float32)
-    return dot(left_high, right_high) + (dot(left_low, right_high) + dot(left_high, right_low))
+    rows = left_high.shape[0]
+    both = dot(jnp.concatenate([left_high, left_low], axis=0), right_high)
+    return both[:rows] + (both[rows:] + dot(left_high, right_low))
 
 
 def farthest_first(size):
@@ -330,28 +332,6 @@
             peer = lax.rem(z + step, nz)
             arrive(far_places[axis].at[peer], r_fz.at[axis, peer])
 
-    def tile_over_y(peer):
-        start = peer * half
-        left = halves(jnp.concatenate(
-            [along_x[panel, group, pl.ds(start, half)].reshape(half * height, width) for panel in (0, 1) for group in range(nx)],
-            axis=1,
-        ))
-        for owner in (0, 1):
-            value = product(left, (high_x[owner], low_x[owner]))
-            sum_x[peer, :, owner] = value.reshape(half, height, qx)
-
-    def tile_over_x(offset):
-        for start in range(0, ny, half):
-            left = halves(jnp.concatenate(
-                [
-                    jnp.concatenate([along_y[panel, group, (start + part) * half + offset] for part in range(half)], axis=0)
-                    for panel in (0, 1) for group in range(ny)
-                ],
-                axis=1,
-            ))
-            for owner in (0, 1):
-                value = product(left, (high_y[owner], low_y[owner]))
-                sum_y[offset, pl.ds(start, half), owner] = value.reshape(half, height, qy)
     y_up, y_down = lax.rem(y + 1, ny), lax.rem(y + ny - 1, ny)
     x_up, x_down = lax.rem(x + 1, nx), lax.rem(x + nx - 1, nx)
     row_up, row_down = y_up * nx + x, y_down * nx + x
@@ -359,88 +339,113 @@
     own_offset = lax.div(x, 2)
     up_offset, down_offset = lax.div(x_up, 2), lax.div(x_down, 2)
     first, last = pl.ds(0, half), pl.ds(half, half)
-
-    @pl.loop(0, 2)
-    def _(step):
-        tile_over_y(jnp.where(step == 0, y_far, y_down))
-
-        @pl.when(step == 0)
-        def _():
-            send(sum_x.at[y_far, 0], relay_x.at[0], s_rx.at[0], r_rx.at[0], row_up, col)
-            send(sum_x.at[y_far, 1], relay_x.at[1], s_rx.at[1], r_rx.at[1], row_down, col)
-
-        @pl.when(step == 1)
-        def _():
-            send(sum_x.at[y_down, 0], land_x.at[1, 0], s_sx.at[1, 0], r_sx.at[1, 0], row_down, col)
-
-        tile_over_x(jnp.where(
-            step == 0, jnp.where(holder, 1 - own_offset, up_offset), jnp.where(holder, own_offset, down_offset)
+    bridge = jnp.logical_not(holder)
+
+    def tile_over_y(peer, owner):
+        left = halves(jnp.concatenate(
+            [
+                along_x[panel, group, pl.ds(peer * half, half)].reshape(half * height, width)
+                for panel in (0, 1) for group in range(nx)
+            ],
+            axis=1,
         ))
-
-        @pl.when(jnp.logical_and(step == 0, holder))
-        def _():
-            send(sum_y.at[1 - own_offset, first], relay_y.at[0], s_ry.at[0], r_ry.at[0], side_up, col)
-            send(sum_y.at[1 - own_offset, last], relay_y.at[1], s_ry.at[1], r_ry.at[1], side_down, col)
-
-        @pl.when(jnp.logical_and(step == 0, jnp.logical_not(holder)))
-        def _():
-            send(sum_y.at[up_offset, last], land_y.at[0, last], s_sy.at[0, 1], r_sy.at[0, 1], side_up, col)
-
-        @pl.when(jnp.logical_and(step == 1, jnp.logical_not(holder)))
-        def _():
-            send(sum_y.at[down_offset, first], land_y.at[1, first], s_sy.at[1, 0], r_sy.at[1, 0], side_down, col)
-
-        @pl.when(step == 1)
-        def _():
-            arrive(relay_x.at[0], r_rx.at[0])
-            sum_x[y_up, 0] = sum_x[y_up, 0] + relay_x[0]
-            send(sum_x.at[y_up, 0], land_x.at[0, 0], s_sx.at[0, 0], r_sx.at[0, 0], row_up, col)
-            arrive(relay_x.at[1], r_rx.at[1])
-            sum_x[y_down, 1] = sum_x[y_down, 1] + relay_x[1]
-            send(sum_x.at[y_down, 1], land_x.at[1, 1], s_sx.at[1, 1], r_sx.at[1, 1], row_down, col)
-
-            @pl.when(jnp.logical_not(holder))
-            def _():
-                arrive(relay_y.at[0], r_ry.at[0])
-                sum_y[up_offset, first] = sum_y[up_offset, first] + relay_y[0]
-                send(sum_y.at[up_offset, first], land_y.at[0, first], s_sy.at[0, 0], r_sy.at[0, 0], side_up, col)
-                arrive(relay_y.at[1], r_ry.at[1])
-                sum_y[down_offset, last] = sum_y[down_offset, last] + relay_y[1]
-                send(sum_y.at[down_offset, last], land_y.at[1, last], s_sy.at[1, 1], r_sy.at[1, 1], side_down, col)
-
-        tile_over_y(jnp.where(step == 0, y_up, y))
-
-        @pl.when(step == 0)
-        def _():
-            send(sum_x.at[y_up, 1], land_x.at[0, 1], s_sx.at[0, 1], r_sx.at[0, 1], row_up, col)
-
-    own_copies[3].wait()
-
-    for offset in range(half):
-        for side in (0, 1):
-            arrive(land_x.at[side, offset], r_sx.at[side, offset])
-        for owner in (0, 1):
-            value = sum_x[y, offset, owner] + land_x[0, offset, owner] + land_x[1, offset, owner]
+        value = product(left, (high_x[owner], low_x[owner]))
+        sum_x[peer, :, owner] = value.reshape(half, height, qx)
+
+    def tile_over_x(offset, start, owner):
+        left = halves(jnp.concatenate(
+            [
+                jnp.concatenate([along_y[panel, group, (start + part) * half + offset] for part in range(half)], axis=0)
+                for panel in (0, 1) for group in range(ny)
+            ],
+            axis=1,
+        ))
+        value = product(left, (high_y[owner], low_y[owner]))
+        sum_y[offset, pl.ds(start, half), owner] = value.reshape(half, height, qy)
+
+    def early(owner):
+        tile_over_x(jnp.where(holder, 1 - own_offset, up_offset), jnp.where(holder, 0, half), owner)
+
+        @pl.when(holder)
+        def _():
+            send(sum_y.at[1 - own_offset, first, owner], relay_y.at[0, :, owner],
+                 s_ry.at[owner, 0], r_ry.at[owner, 0], side_up, col)
+
+        @pl.when(bridge)
+        def _():
+            send(sum_y.at[up_offset, last, owner], land_y.at[0, last, owner],
+                 s_sy.at[owner, 0, 1], r_sy.at[owner, 0, 1], side_up, col)
+
+        tile_over_y(y_far, owner)
+        send(sum_x.at[y_far, 0, owner], relay_x.at[0, owner], s_rx.at[owner, 0], r_rx.at[owner, 0], row_up, col)
+        send(sum_x.at[y_far, 1, owner], relay_x.at[1, owner], s_rx.at[owner, 1], r_rx.at[owner, 1], row_down, col)
+
+        tile_over_x(jnp.where(holder, 1 - own_offset, down_offset), jnp.where(holder, half, 0), owner)
+
+        @pl.when(holder)
+        def _():
+            send(sum_y.at[1 - own_offset, last, owner], relay_y.at[1, :, owner],
+                 s_ry.at[owner, 1], r_ry.at[owner, 1], side_down, col)
+
+        @pl.when(bridge)
+        def _():
+            send(sum_y.at[down_offset, first, owner], land_y.at[1, first, owner],
+                 s_sy.at[owner, 1, 0], r_sy.at[owner, 1, 0], side_down, col)
+
+        tile_over_y(y_up, owner)
+        send(sum_x.at[y_up, 1, owner], land_x.at[0, 1, owner], s_sx.at[owner, 0, 1], r_sx.at[owner, 0, 1], row_up, col)
+        tile_over_y(y_down, owner)
+        send(sum_x.at[y_down, 0, owner], land_x.at[1, 0, owner], s_sx.at[owner, 1, 0], r_sx.at[owner, 1, 0], row_down, col)
+
+    def late(owner):
+        tile_over_x(jnp.where(holder, own_offset, up_offset), 0, owner)
+
+        @pl.when(bridge)
+        def _():
+            arrive(relay_y.at[0, :, owner], r_ry.at[owner, 0])
+            sum_y[up_offset, first, owner] = sum_y[up_offset, first, owner] + relay_y[0, :, owner]
+            send(sum_y.at[up_offset, first, owner], land_y.at[0, first, owner],
+                 s_sy.at[owner, 0, 0], r_sy.at[owner, 0, 0], side_up, col)
+
+        arrive(relay_x.at[0, owner], r_rx.at[owner, 0])
+        sum_x[y_up, 0, owner] = sum_x[y_up, 0, owner] + relay_x[0, owner]
+        send(sum_x.at[y_up, 0, owner], land_x.at[0, 0, owner], s_sx.at[owner, 0, 0], r_sx.at[owner, 0, 0], row_up, col)
+        arrive(relay_x.at[1, owner], r_rx.at[owner, 1])
+        sum_x[y_down, 1, owner] = sum_x[y_down, 1, owner] + relay_x[1, owner]
+        send(sum_x.at[y_down, 1, owner], land_x.at[1, 1, owner], s_sx.at[owner, 1, 1], r_sx.at[owner, 1, 1], row_down, col)
+
+        tile_over_x(jnp.where(holder, own_offset, down_offset), half, owner)
+
+        @pl.when(bridge)
+        def _():
+            arrive(relay_y.at[1, :, owner], r_ry.at[owner, 1])
+            sum_y[down_offset, last, owner] = sum_y[down_offset, last, owner] + relay_y[1, :, owner]
+            send(sum_y.at[down_offset, last, owner], land_y.at[1, last, owner],
+                 s_sy.at[owner, 1, 1], r_sy.at[owner, 1, 1], side_down, col)
+
+        tile_over_y(y, owner)
+
+    def finish(owner):
+        for offset in range(half):
+            for side in (0, 1):
+                arrive(land_x.at[side, offset, owner], r_sx.at[owner, side, offset])
+            done_x[offset, owner] = sum_x[y, offset, owner] + land_x[0, offset, owner] + land_x[1, offset, owner]
             target = 2 * offset + core
-            here = jnp.logical_and(target == x, owner == core)
-            done_x[offset, owner] = value
-
-            @pl.when(jnp.logical_not(here))
+
+            @pl.when(jnp.logical_not(jnp.logical_and(target == x, owner == core)))
             def _():
                 send(
                     done_x.at[offset, owner], tile_x.at[x], s_tx.at[offset, owner], r_tx.at[x],
                     y * nx + target, 2 * z + owner,
                 )
 
-    @pl.when(holder)
-    def _():
-        for peer in range(ny):
-            if peer % half == 0:
-                for side in (0, 1):
-                    arrive(land_y.at[side, pl.ds(peer, half)], r_sy.at[side, peer // half])
-            for owner in (0, 1):
-                value = sum_y[own_offset, peer, owner] + land_y[0, peer, owner] + land_y[1, peer, owner]
-                done_y[peer, owner] = value
+        @pl.when(holder)
+        def _():
+            for peer in range(ny):
+                if peer % half == 0:
+                    for side in (0, 1):
+                        arrive(land_y.at[side, pl.ds(peer, half), owner], r_sy.at[owner, side, peer // half])
+                done_y[peer, owner] = sum_y[own_offset, peer, owner] + land_y[0, peer, owner] + land_y[1, peer, owner]
 
                 @pl.when(jnp.logical_not(jnp.logical_and(peer == y, owner == core)))
                 def _():
@@ -449,7 +454,17 @@
                         peer * nx + x, 2 * z + owner,
                     )
 
-        tile_x[x] = done_x[lax.div(x, 2), core]
+    early(0)
+    late(0)
+    early(1)
+    finish(0)
+    late(1)
+    finish(1)
+    own_copies[3].wait()
+
+    @pl.when(holder)
+    def _():
+        tile_x[x] = done_x[own_offset, core]
         tile_y[y] = done_y[y, core]
 
     for group in range(nx):
@@ -536,18 +551,19 @@
         for step in z_steps:
             sent(own_block, s_fz.at[axis, lax.rem(z + step, nz)])
 
-    for side in (0, 1):
-        sent(relay_x.at[0], s_rx.at[side])
-        for piece in (0, 1):
-            sent(land_x.at[0, 0], s_sx.at[side, piece])
-
-            @pl.when(jnp.logical_not(holder))
-            def _():
-                sent(land_y.at[0, first], s_sy.at[side, piece])
-
-        @pl.when(holder)
-        def _():
-            sent(relay_y.at[0], s_ry.at[side])
+    for owner in (0, 1):
+        for side in (0, 1):
+            sent(relay_x.at[0, 0], s_rx.at[owner, side])
+            for piece in (0, 1):
+                sent(land_x.at[0, 0, 0], s_sx.at[owner, side, piece])
+
+                @pl.when(bridge)
+                def _():
+                    sent(land_y.at[0, first, 0], s_sy.at[owner, side, piece])
+
+            @pl.when(holder)
+            def _():
+                sent(relay_y.at[0, :, 0], s_ry.at[owner, side])
 
     @pl.when(holder)
     def _():
@@ -616,7 +632,7 @@
             dma(2, nz), dma(2, nz), dma(2, nz), dma(2, nz),
             dma(2, nx), dma(2, nx), dma(2, ny), dma(2, ny), dma(2, 2), dma(2, 2),
             dma(2, 2, nx), dma(2, 2, nx), dma(2, 2, ny), dma(2, 2, ny),
-            dma(2, 2), dma(2, 2), dma(2, 2), dma(2, 2), dma(2), dma(2), dma(2), dma(2),
+            dma(2, 2, 2), dma(2, 2, 2), dma(2, 2, 2), dma(2, 2, 2), dma(2, 2), dma(2, 2), dma(2, 2), dma(2, 2),
             dma(2), dma(2), dma(2, nz), dma(2, nz),
             dma(half, 2), dma(nx), dma(ny, 2), dma(ny),
             dma(2), dma(2),

time: 116 us -> 111 us (0.957); the launches traced: 115 us -> 111 us
  Pallas kernels: 112 us -> 109 us
    pallas_call x1, Pallas kernels: 112 us -> 109 us  [local(): pl.pallas_call(functools.partial(solve_kernel, (rows, nx, ny, nz, height,...]
where the time goes in v5:
time: 111 us
  Pallas kernels  109 us (98%)
  local copies, waits for them, and re-layouts  1.94 us (2%)
    pallas_call x1, Pallas kernels, local(): pl.pallas_call(functools.partial(solve_kernel, (rows, nx, ny, nz, height,...  109 us

profile of v5, /device:TPU:1, one launch (start us, length us, event | category | flops | bytes accessed | tf_op | source)
XLA Modules:
  0.0 111.2 jit_solution(10114009441476401864)
XLA Ops:
  0.6 108.6 %shard_map.68 = (f32[2,8,2,64,128]{4,3,2,1,0:T(8,128)S(1)}, f32[64,4096]{1,0:T(8,128)S(1)}) custom-call(f32[2,128,128]{2,1,0:T(8,128)} %diag_hbm.1, f32[128,128]{1,0:T(8,128)} %cross_hbm.1, f32[2,128,4096]{2,1,0:T(8,128)} %coupling_hbm.1, f32[2,64,128]{2,1,0:T(8,128)} %loads_hbm.1, f32[64,4096]{1,0:T(8,128)} %rest_hbm.1), custom_call_target="tpu_custom_call" | custom-call | tf_op jit(solution)/shard_map/pallas_call | solution.py:589
  109.3 1.0 copy.9
  110.2 1.0 copy.10

commit v6 on v5

--- a/solution.py
+++ b/solution.py
@@ -104,19 +104,15 @@
 
     barrier = pltpu.get_barrier_semaphore()
 
-    @pl.loop(0, rows)
-    def _(step):
-        peer = lax.rem(row + step, rows)
-        pl.semaphore_signal(barrier, inc=1, device_id={"row": peer, "col": sibling}, device_id_type=MESH)
-
-        @pl.when(step > 0)
-        def _():
-            pl.semaphore_signal(barrier, inc=1, device_id={"row": peer, "col": col}, device_id_type=MESH)
-
-    @pl.loop(1, nz)
-    def _(step):
-        peer = lax.rem(z + step, nz)
-        pl.semaphore_signal(barrier, inc=1, device_id={"row": row, "col": 2 * peer + core}, device_id_type=MESH)
+    def greet(to_row, to_col):
+        pl.semaphore_signal(barrier, inc=1, device_id={"row": to_row, "col": to_col}, device_id_type=MESH)
+
+    for step in z_steps:
+        greet(row, 2 * lax.rem(z + step, nz) + core)
+    for step in plane_steps:
+        greet(beside(step), col)
+        greet(beside(step), sibling)
+    greet(row, sibling)
 
     pl.semaphore_wait(barrier, 2 * rows - 1 + nz - 1)
 
@@ -318,19 +314,18 @@
     split_dealt(1)
     split_dealt(0)
 
-    for h in (0, 1):
-        for panel in (1, 0):
-            for step in x_steps[panel:]:
-                peer = lax.rem(x + step, nx)
-                arrive(along_x.at[panel, peer, :, rows_of(h)], r_lx.at[h, panel, peer])
-            for step in y_steps[panel:]:
-                peer = lax.rem(y + step, ny)
-                arrive(along_y.at[panel, peer, :, rows_of(h)], r_ly.at[h, panel, peer])
-
-    for axis in (0, 1):
+    def await_solved(axis):
+        along, me, size, steps, recv = (
+            (along_x, x, nx, x_steps, r_lx), (along_y, y, ny, y_steps, r_ly)
+        )[axis]
         for step in z_steps:
             peer = lax.rem(z + step, nz)
             arrive(far_places[axis].at[peer], r_fz.at[axis, peer])
+        for h in (0, 1):
+            for panel in (1, 0):
+                for step in steps[panel:]:
+                    peer = lax.rem(me + step, size)
+                    arrive(along.at[panel, peer, :, rows_of(h)], recv.at[h, panel, peer])
 
     y_up, y_down = lax.rem(y + 1, ny), lax.rem(y + ny - 1, ny)
     x_up, x_down = lax.rem(x + 1, nx), lax.rem(x + nx - 1, nx)
@@ -364,6 +359,8 @@
         sum_y[offset, pl.ds(start, half), owner] = value.reshape(half, height, qy)
 
     def early(owner):
+        if owner == 0:
+            await_solved(1)
         tile_over_x(jnp.where(holder, 1 - own_offset, up_offset), jnp.where(holder, 0, half), owner)
 
         @pl.when(holder)
@@ -376,6 +373,8 @@
             send(sum_y.at[up_offset, last, owner], land_y.at[0, last, owner],
                  s_sy.at[owner, 0, 1], r_sy.at[owner, 0, 1], side_up, col)
 
+        if owner == 0:
+            await_solved(0)
         tile_over_y(y_far, owner)
         send(sum_x.at[y_far, 0, owner], relay_x.at[0, owner], s_rx.at[owner, 0], r_rx.at[owner, 0], row_up, col)
         send(sum_x.at[y_far, 1, owner], relay_x.at[1, owner], s_rx.at[owner, 1], r_rx.at[owner, 1], row_down, col)

time: 111 us -> 111 us (level)
  no operation moved by 1% of the time
where the time goes in v6:
time: 111 us; the launch traced here: 110 us
  Pallas kernels  108 us (97%)
  local copies, waits for them, and re-layouts  1.94 us (2%)
    pallas_call x1, Pallas kernels, local(): pl.pallas_call(functools.partial(solve_kernel, (rows, nx, ny, nz, height,...  108 us

profile of v6, /device:TPU:1, one launch (start us, length us, event | category | flops | bytes accessed | tf_op | source)
XLA Modules:
  0.0 110.3 jit_solution(15516232228106952134)
XLA Ops:
  0.6 107.7 %shard_map.68 = (f32[2,8,2,64,128]{4,3,2,1,0:T(8,128)S(1)}, f32[64,4096]{1,0:T(8,128)S(1)}) custom-call(f32[2,128,128]{2,1,0:T(8,128)} %diag_hbm.1, f32[128,128]{1,0:T(8,128)} %cross_hbm.1, f32[2,128,4096]{2,1,0:T(8,128)} %coupling_hbm.1, f32[2,64,128]{2,1,0:T(8,128)} %loads_hbm.1, f32[64,4096]{1,0:T(8,128)} %rest_hbm.1), custom_call_target="tpu_custom_call" | custom-call | tf_op jit(solution)/shard_map/pallas_call | solution.py:588
  108.3 1.0 copy.9
  109.3 1.0 copy.10

commit v7 on v6

--- a/solution.py
+++ b/solution.py
@@ -90,17 +90,10 @@
             coupling_hbm.at[:, :, pl.ds(pl.multiple_of(nx * qx + y * qy, qy), qy)], raw_y.at[core, :, y], local_sem.at[5]
         ),
     ]
-    for copy in own_copies:
-        copy.start()
     own_upper = [
         pltpu.make_async_copy(loads_hbm.at[1, pl.ds(h * part, part)], gathered.at[h, slot, core], local_sem.at[6 + h])
         for h in (0, 1)
     ]
-
-    @pl.when(holder)
-    def _():
-        for copy in own_upper:
-            copy.start()
 
     barrier = pltpu.get_barrier_semaphore()
 
@@ -113,6 +106,14 @@
         greet(beside(step), col)
         greet(beside(step), sibling)
     greet(row, sibling)
+
+    for copy in own_copies:
+        copy.start()
+
+    @pl.when(holder)
+    def _():
+        for copy in own_upper:
+            copy.start()
 
     pl.semaphore_wait(barrier, 2 * rows - 1 + nz - 1)
 

time: 111 us -> 110 us (level)
  no operation moved by 1% of the time
where the time goes in v7:
time: 110 us
  Pallas kernels  108 us (98%)
  local copies, waits for them, and re-layouts  1.94 us (2%)
    pallas_call x1, Pallas kernels, local(): pl.pallas_call(functools.partial(solve_kernel, (rows, nx, ny, nz, height,...  108 us

profile of v7, /device:TPU:1, one launch (start us, length us, event | category | flops | bytes accessed | tf_op | source)
XLA Modules:
  0.0 110.1 jit_solution(4701521332885616840)
XLA Ops:
  0.6 107.5 %shard_map.68 = (f32[2,8,2,64,128]{4,3,2,1,0:T(8,128)S(1)}, f32[64,4096]{1,0:T(8,128)S(1)}) custom-call(f32[2,128,128]{2,1,0:T(8,128)} %diag_hbm.1, f32[128,128]{1,0:T(8,128)} %cross_hbm.1, f32[2,128,4096]{2,1,0:T(8,128)} %coupling_hbm.1, f32[2,64,128]{2,1,0:T(8,128)} %loads_hbm.1, f32[64,4096]{1,0:T(8,128)} %rest_hbm.1), custom_call_target="tpu_custom_call" | custom-call | tf_op jit(solution)/shard_map/pallas_call | solution.py:589
  108.1 1.0 copy.9
  109.1 1.0 copy.10
